TPU v7x, 128 devices: a whole 4x4x4 slice. The times are simulated.
128 devices in a mesh: req: 4 (over z), vocab: 32 (over y, x, core).
Axes of the slice: x: 4, y: 4, z: 4, core: 2. Of those that a mesh axis runs over, the one named last changes fastest.
Arguments:
- hidden_states: bfloat16 [24576, 2048], P(('req', 'vocab')), may hold values from -400 to 400
- norm_gain: float32 [2048], replicated, may hold values from 0.25 to 1.75
- head_weight: bfloat16 [2048, 32000], P(None, 'vocab'), may hold values from -2 to 2
- targets: int32 [24576], P(('req', 'vocab')), may hold values from 0 to 31999
- lengths: int32 [1024], P(('req', 'vocab')), may hold values from 1 to 24, as said below
- slot_of: int32 [1024], P(('req', 'vocab')), may hold values from 0 to 1023, each once
Outputs:
- logprob: float32 [1024, 24], P(('req', 'vocab'))
- entropy: float32 [1024, 24], P(('req', 'vocab'))
Inputs may be any that keep to these rules, and one draw needn't show every extreme that they name: The lengths of the 8 requests of one device sum to at most 128; some device's sum to exactly 128.
All inputs are finite; a program needn't handle non-finite values.
Results may differ from a plain program's by a relative error of at most 0.00097.
Values may be sent and summed in bfloat16 or wider, within the bound.
A program may use at most 128 MiB of HBM per device.

v0:
```python
import jax
import jax.numpy as jnp
from jax import lax
from jax.sharding import PartitionSpec as P

eps_norm = 1e-05
block_rows = 512


def normalize(hidden_rows, norm_gain):
    values = hidden_rows.astype(jnp.float32)
    inverse_rms = lax.rsqrt(jnp.mean(values * values, axis=1, keepdims=True) + eps_norm)
    return (values * inverse_rms * norm_gain[None, :]).astype(jnp.bfloat16)


def piece_stats(piece_rows, piece_targets, head_weight, vocab_start):
    logits = jnp.dot(piece_rows, head_weight, preferred_element_type=jnp.float32)
    row_peak = jnp.max(logits, axis=1)
    shifted = logits - row_peak[:, None]
    exponent = jnp.exp(shifted)
    row_total = jnp.sum(exponent, axis=1)
    spread = jnp.sum(exponent * shifted, axis=1)
    column = lax.broadcasted_iota(jnp.int32, logits.shape, 1) + vocab_start
    picked = jnp.sum(jnp.where(column == piece_targets[:, None], logits, 0.0), axis=1)
    return (row_peak, row_total, spread, picked)


def blocked_stats(piece_rows, piece_targets, head_weight, vocab_start):
    row_count = piece_rows.shape[0]

    def one_block(block_pair):
        return piece_stats(block_pair[0], block_pair[1], head_weight, vocab_start)

    stacked = lax.map(
        one_block,
        (
            piece_rows.reshape(row_count // block_rows, block_rows, piece_rows.shape[1]),
            piece_targets.reshape(row_count // block_rows, block_rows),
        ),
    )
    return tuple((stat_block.reshape(row_count) for stat_block in stacked))


def rescale(group_stats, peak_all):
    row_peak, row_total, spread, picked = group_stats
    factor = jnp.exp(row_peak - peak_all)
    return (row_total * factor, factor * (spread + (row_peak - peak_all) * row_total), picked)


def local(hidden_states, norm_gain, head_weight, targets, lengths, slot_of):
    seq_count = lengths.shape[0]
    seq_len = hidden_states.shape[0] // seq_count
    vocab_index = lax.axis_index("vocab")
    vocab_start = vocab_index * head_weight.shape[1]
    position = lax.broadcasted_iota(jnp.int32, (seq_count, seq_len), 1)
    live_mask = position < lengths[:, None]
    held_rows = seq_count * seq_len
    sent_rows = normalize(hidden_states, norm_gain)
    fresh = blocked_stats(
        lax.all_gather(sent_rows, "vocab", axis=0, tiled=True),
        lax.all_gather(targets, "vocab", axis=0, tiled=True),
        head_weight,
        vocab_start,
    )
    group_stats = tuple((new_part for new_part in fresh))
    owner_start = vocab_index * held_rows
    peak_all = lax.pmax(group_stats[0], "vocab")
    scaled_total, scaled_spread, picked_all = rescale(group_stats, peak_all)
    summed = lax.psum((scaled_total, scaled_spread, picked_all), "vocab")
    row_total, spread, picked = tuple(
        (lax.dynamic_slice_in_dim(summed_part, owner_start, held_rows) for summed_part in summed)
    )
    global_peak = lax.dynamic_slice_in_dim(peak_all, owner_start, held_rows)
    log_total = jnp.log(row_total)
    own_logprob = picked - global_peak - log_total
    own_entropy = log_total - spread / row_total
    slot_logprob = own_logprob.reshape(seq_count, seq_len)
    slot_entropy = own_entropy.reshape(seq_count, seq_len)
    slot_logprob = jnp.where(live_mask, slot_logprob, 0.0)
    slot_entropy = jnp.where(live_mask, slot_entropy, 0.0)
    all_logprob, all_entropy = (
        lax.all_gather(slot_logprob, ("req", "vocab"), axis=0, tiled=True),
        lax.all_gather(slot_entropy, ("req", "vocab"), axis=0, tiled=True),
    )
    return (all_logprob[slot_of], all_entropy[slot_of])


def solution(mesh):
    in_specs = (
        P(("req", "vocab"), None),
        P(),
        P(None, "vocab"),
        P(("req", "vocab")),
        P(("req", "vocab")),
        P(("req", "vocab")),
    )
    out_specs = (P(("req", "vocab"), None), P(("req", "vocab"), None))
    return jax.shard_map(local, mesh=mesh, in_specs=in_specs, out_specs=out_specs, check_vma=False)
```

profile of v0, /device:TPU:1, one launch (start us, length us, event | category | flops | bytes accessed | tf_op | source)
XLA Modules:
  0.0 517.9 jit_solution(5744212127510986810)
XLA Ops:
  7.2 1.4 fusion.5
  8.6 2.3 fusion.7
  11.1 0.6 dynamic-slice
  12.3 0.3 dynamic-update-slice
  12.6 127.5 %all-reduce = s32[6144]{0:T(1024)S(1)} all-reduce(s32[6144]{0:T(1024)S(1)} %dynamic-update-slice), channel_id=1, replica_groups=mesh['req'=4,'vocab'=32] {'vocab'}, use_global_device_ids=true, to_apply=%add | all-reduce | flops 6144 | bytes 49152
  140.2 72.9 %while.16 = (s32[]{:T(128)}, f32[12,512]{1,0:T(8,128)S(1)}, f32[12,512]{1,0:T(8,128)S(1)}, f32[12,512]{1,0:T(8,128)S(1)}, f32[12,512]{1,0:T(8,128)S(1)}, /*index...) while((s32[]{:T(128)}, f32[12,512]{1,0:T(8,128)S(1)}, ...), condition=%wide.region_6.7_spmd, body=%wide.region_1.6_spmd.sunk | while | flops 2101246976 | bytes 10330565 | solution.py:34
  140.2 5.1 fusion.16
  145.3 0.6 fusion.17
  146.0 0.1 dynamic_update_slice.20
  146.3 5.1 fusion.16
  151.4 0.6 fusion.17
  152.1 0.1 dynamic_update_slice.20
  152.2 0.1 dynamic_update_slice.18
  152.3 5.1 fusion.16
  157.5 0.6 fusion.17
  158.2 0.1 dynamic_update_slice.20
  158.2 0.1 dynamic_update_slice.18
  158.4 5.1 fusion.16
  163.5 0.6 fusion.17
  164.2 0.1 dynamic_update_slice.20
  164.5 5.1 fusion.16
  169.6 0.6 fusion.17
  170.5 5.1 fusion.16
  175.7 0.6 fusion.17
  176.6 5.1 fusion.16
  181.8 0.6 fusion.17
  182.7 5.1 fusion.16
  187.8 0.6 fusion.17
  188.8 5.1 fusion.16
  193.9 0.6 fusion.17
  194.8 5.1 fusion.16
  200.0 0.6 fusion.17
  200.9 5.1 fusion.16
  206.0 0.6 fusion.17
  207.0 5.1 fusion.16
  212.1 0.6 fusion.17
  213.0 123.8 %pmax.7 = f32[6144]{0:T(1024)S(1)} all-reduce(f32[6144]{0:T(1024)S(1)} %reshape.44), channel_id=1, replica_groups=mesh['req'=4,'vocab'=32] {'vocab'}, use_global_device_ids=true, to_apply=%region_8.9 | all-reduce | flops 6144 | bytes 49152 | tf_op jit(solution)/shard_map/pmax | solution.py:67
  336.8 0.6 reshape.43
  337.4 0.6 add_multiply_fusion
  338.1 100.9 %all-reduce.4.cloned.1.call-done = (f32[6144]{0:T(1024)}, f32[6144]{0:T(1024)}, f32[6144]{0:T(1024)}) async-done(((f32[6144]{0:T(1024)}, f32[6144]{0:T(1024)}, f32[6144]{0:T(1024)}), (f32[6144]{0:T(1024)}, f32[6144]{0:T(1024)}, f32[6144]{0:T(1024)})) %all-reduce.4.cloned.1.call-update) | async-done | bytes 73744 | tf_op jit(solution)/shard_map/psum | solution.py:69
  439.1 0.8 divide_subtract_fusion
  439.9 0.1 reshape.46
  439.9 0.1 reshape.48
  440.0 0.1 fusion.8
  440.1 34.7 %all_gather.14 = f32[1024,24]{1,0:T(8,128)S(1)} all-gather(f32[8,24]{1,0:T(8,128)S(1)} %get-tuple-element.87), channel_id=1, replica_groups=mesh['req'=4,'vocab'=32] {'req','vocab'}, dimensions={0}, use_global_device_ids=true | all-gather | bytes 99072 | tf_op jit(solution)/shard_map/all_gather | solution.py:82
  474.8 33.9 %all_gather.15 = f32[1024,24]{1,0:T(8,128)S(1)} all-gather(f32[8,24]{1,0:T(8,128)S(1)} %get-tuple-element.86), channel_id=1, replica_groups=mesh['req'=4,'vocab'=32] {'req','vocab'}, dimensions={0}, use_global_device_ids=true | all-gather | bytes 99072 | tf_op jit(solution)/shard_map/all_gather | solution.py:83
  508.7 1.1 gather_fusion
  509.9 1.1 gather_fusion.1
  (91 shorter events, 3.0 us)
Async XLA Ops:
  7.2 3.9 copy-start.3
  7.2 5.2 copy-start
  7.2 132.9 %copy-start.2 = (s32[8]{0:T(128)S(1)}, s32[8]{0:T(128)}, u32[]{:S(2)}) copy-start(s32[8]{0:T(128)} %param.13) | copy-start | bytes 100
  7.2 133.0 %all-gather.2.cloned.1.call-start = ((), (), s32[]{:S(2)}) async-start(), calls=%async_computation | async-start | bytes 25952256 | tf_op jit(solution)/shard_map/all_gather | solution.py:60
  11.0 428.1 %all-reduce.4.cloned.1.call-start = ((), (), s32[]{:S(2)}) async-start(), calls=%async_computation.1 | async-start | bytes 147456 | tf_op jit(solution)/shard_map/psum | solution.py:69
  140.2 299.9 %copy-start.1 = (s32[8]{0:T(128)S(1)}, s32[8]{0:T(128)}, u32[]{:S(2)}) copy-start(s32[8]{0:T(128)} %param.12) | copy-start | bytes 100
Sparse Core Ops, SparseCore 0:
  11.1 95.8 all-gather.1
  338.2 100.7 all-reduce.3
where the time goes:
time: 518 us
  blocking collectives  320 us (62%)
  waiting for transfers between devices  101 us (19%)
  matrix products  61.4 us (12%)
  between operations  14.8 us (3%)
  other arithmetic  12.7 us (2%)
  local copies, waits for them, and re-layouts  7.11 us (1%)
    unnamed x1, blocking collectives  127 us
    pmax x1, blocking collectives, local(): peak_all = lax.pmax(group_stats[0], 'vocab')  124 us
    psum x1, waiting for transfers between devices, local(): summed = lax.psum((scaled_total, scaled_spread, picked_all), 'vocab')  101 us
    dot_general x12, matrix products, piece_stats(): jnp.dot(piece_rows, head_weight, preferred_element_type=jnp.float32)  61.4 us
    all_gather x1, blocking collectives, local(): lax.all_gather(slot_logprob, ('req', 'vocab'), axis=0, tiled=True)  34.7 us
    all_gather x1, blocking collectives, local(): lax.all_gather(slot_entropy, ('req', 'vocab'), axis=0, tiled=True)  33.9 us
  transfers between devices with their start and end apart: 2, of which 1 were waited for; matrix products, arithmetic and copies ran while one was open for 0% of the time, Pallas kernels for 0%

commit v1 on v0

v1 whole, which is shorter than its diff:
```python
import jax
import jax.numpy as jnp
from jax import lax
from jax.experimental import pallas as pl
from jax.experimental.pallas import tpu as pltpu

eps_norm = 1e-05
side = 4
cap = 128
pieces = 2
piece_rows = cap // pieces
mesh_ids = pl.DeviceIdType.MESH
f32 = jnp.float32

group_order = [(0, 0), (0, 1), (1, 0), (0, 3), (3, 0), (0, 2), (2, 0), (1, 1), (1, 3), (3, 1), (3, 3),
               (2, 1), (1, 2), (2, 3), (3, 2), (2, 2)]
slot_at = {group: index for index, group in enumerate(group_order)}
arrivals = [
    [],
    [(0, 1, 0), (0, 3, 0), (1, 0, 0), (3, 0, 0), (0, 1, 1), (0, 3, 1), (1, 0, 1), (3, 0, 1)],
    [], [],
    [(1, 1, 0), (0, 2, 0), (2, 0, 0)],
    [(2, 0, 1), (1, 3, 0), (3, 1, 0), (0, 2, 1), (3, 3, 0)],
    [(1, 1, 1), (1, 3, 1)],
    [(3, 1, 1)],
    [(3, 3, 1)],
    [(2, 1, 0)],
    [(2, 3, 0)],
    [(2, 1, 1), (2, 3, 1), (1, 2, 0), (1, 2, 1)],
    [],
    [(3, 2, 0), (3, 2, 1)],
    [],
    [(2, 2, 0), (2, 2, 1)],
]
links = [(1, 0), (3, 0), (0, 1), (0, 3)]


def onward(da, db, part):
    first_half = part < pieces // 2
    taken = []
    if db == 0:
        if da == 0 or (da == 3 and first_half):
            taken.append(0)
        if da == 0 or (da == 1 and not first_half):
            taken.append(1)
        taken += [2, 3]
    else:
        if db == 3 and first_half:
            taken.append(2)
        if db == 1 and not first_half:
            taken.append(3)
    return taken


send_count = 0
send_plan = {}
for arrival_group in group_order:
    for arrival_part in range(pieces):
        for link_taken in ["partner"] + onward(*arrival_group, arrival_part):
            send_plan[(arrival_group, arrival_part, link_taken)] = send_count
            send_count += 1


def kernel(lens, slots, hidden, gain, targets, weight_hbm, out_logprob, out_entropy,
           weight, weight_t, rows, tags, tag_out, own_stats, stats_in, fin, gathered,
           weight_sem, send_sem, arrive_sem, partner_sem, tag_send, tag_recv,
           stat_send, stat_recv, z_send, z_recv, fin_send, fin_recv):
    req = lax.axis_index("req")
    me = lax.axis_index("vocab")
    core = lax.rem(me, 2)
    chip_x = lax.rem(me // 2, side)
    chip_y = me // (2 * side)
    members = 2 * side * side
    columns = weight.shape[1]

    def device_at(da, db, other):
        x = lax.rem(chip_x + da * (1 - core) + db * core, side)
        y = lax.rem(chip_y + db * (1 - core) + da * core, side)
        the_core = (1 - core) if other else core
        return (y * side + x) * 2 + the_core

    barrier = pltpu.get_barrier_semaphore()

    def greet(step, carry):
        pl.semaphore_signal(barrier, inc=1, device_id=(req, lax.rem(me + step, members)), device_id_type=mesh_ids)
        return carry

    lax.fori_loop(1, members, greet, 0)
    for step in range(1, side):
        pl.semaphore_signal(barrier, inc=1, device_id=(lax.rem(req + step, side), me), device_id_type=mesh_ids)

    weight_copy = pltpu.make_async_copy(weight_hbm, weight, weight_sem)
    weight_copy.start()

    seq_count = lens.shape[0]
    held = hidden.shape[0]
    seq_len = held // seq_count
    offsets = []
    running = jnp.int32(0)
    for seq in range(seq_count):
        offsets.append(running)
        running = running + lens[seq]

    def compact_place(slot_index):
        place = jnp.full(slot_index.shape, -1, jnp.int32)
        for seq in range(seq_count):
            ahead = slot_index - seq * seq_len
            place = jnp.where((ahead >= 0) & (ahead < lens[seq]), ahead + offsets[seq], place)
        return place

    place_row = compact_place(lax.broadcasted_iota(jnp.int32, (8, held), 1))[:1]
    pick = (lax.broadcasted_iota(jnp.int32, (cap, held), 0) == place_row).astype(f32).astype(jnp.bfloat16)
    live = jnp.dot(pick, hidden[...], preferred_element_type=f32)
    inverse_rms = lax.rsqrt(jnp.mean(live * live, axis=1, keepdims=True) + eps_norm)
    rows[0, 0:cap, :] = (live * inverse_rms * gain[...]).astype(jnp.bfloat16)

    place_col = compact_place(lax.broadcasted_iota(jnp.int32, (held, cap), 0))
    pick_t = (lax.broadcasted_iota(jnp.int32, (held, cap), 1) == place_col).astype(f32).astype(jnp.bfloat16)
    wide = targets[...]
    high = wide // 256
    digits = jnp.concatenate([high, wide - high * 256] + [jnp.zeros_like(wide)] * 14, axis=0)
    digits = digits.astype(f32).astype(jnp.bfloat16)
    tag_pair = jnp.dot(digits, pick_t, preferred_element_type=f32)
    tag_own = (tag_pair[0:1] * 256.0 + tag_pair[1:2]).astype(jnp.int32)
    tag_out[0] = tag_own
    tags[me] = tag_own

    pl.semaphore_wait(barrier, members - 1 + side - 1)

    def piece_copy(group, part, link):
        da, db = group
        source = rows.at[slot_at[group], pl.ds(part * piece_rows, piece_rows), :]
        if link == "partner":
            return pltpu.make_async_remote_copy(
                src_ref=source,
                dst_ref=rows.at[slot_at[(db, da)], pl.ds(cap + part * piece_rows, piece_rows), :],
                send_sem=send_sem.at[send_plan[(group, part, link)]],
                recv_sem=partner_sem.at[slot_at[(db, da)] * pieces + part],
                device_id=(req, device_at(0, 0, True)), device_id_type=mesh_ids)
        ma, mb = links[link]
        landing = slot_at[((da - ma) % side, (db - mb) % side)]
        return pltpu.make_async_remote_copy(
            src_ref=source,
            dst_ref=rows.at[landing, pl.ds(part * piece_rows, piece_rows), :],
            send_sem=send_sem.at[send_plan[(group, part, link)]],
            recv_sem=arrive_sem.at[landing * pieces + part],
            device_id=(req, device_at(ma, mb, False)), device_id_type=mesh_ids)

    def arrived(slot, part):
        here = rows.at[slot, pl.ds(part * piece_rows, piece_rows), :]
        return pltpu.make_async_copy(here, here, arrive_sem.at[slot * pieces + part])

    def send_onward(da, db, part):
        for link in onward(da, db, part):
            piece_copy((da, db), part, link).start()
        piece_copy((da, db), part, "partner").start()

    for part in range(pieces):
        send_onward(0, 0, part)

    def tag_copy(step):
        return pltpu.make_async_remote_copy(
            src_ref=tag_out.at[0], dst_ref=tags.at[me], send_sem=tag_send, recv_sem=tag_recv,
            device_id=(req, lax.rem(me + step, members)), device_id_type=mesh_ids)

    def send_tag(step, carry):
        tag_copy(step).start()
        return carry

    lax.fori_loop(1, members, send_tag, 0)

    weight_copy.wait()
    depth = weight.shape[0]
    chunk = 256

    def turn(step, carry):
        start = pl.multiple_of(step * chunk, chunk)
        weight_t[:, pl.ds(start, chunk)] = weight[pl.ds(start, chunk), :].T
        return carry

    lax.fori_loop(0, depth // chunk, turn, 0)

    pltpu.make_async_copy(tags.at[pl.ds(0, members - 1)], tags.at[pl.ds(0, members - 1)], tag_recv).wait()

    def stat_copy(group, other):
        owner = device_at(group[0], group[1], other)
        index = slot_at[group] * 2 + other
        return pltpu.make_async_remote_copy(
            src_ref=own_stats.at[slot_at[group], other], dst_ref=stats_in.at[me],
            send_sem=stat_send.at[index], recv_sem=stat_recv,
            device_id=(req, owner), device_id_type=mesh_ids)

    first_column = me * columns

    def one_group(step, carry):
        for index in range(len(group_order)):
            if arrivals[index]:
                @pl.when(step == index)
                def _():
                    for da, db, part in arrivals[index]:
                        arrived(slot_at[(da, db)], part).wait()
                        send_onward(da, db, part)

        for part in range(pieces):
            there = rows.at[step, pl.ds(cap + part * piece_rows, piece_rows), :]
            pltpu.make_async_copy(there, there, partner_sem.at[step * pieces + part]).wait()

        logits = lax.dot_general(weight_t[...], rows[step], (((1,), (1,)), ((), ())), preferred_element_type=f32)
        da = jnp.int32(0)
        db = jnp.int32(0)
        for index, group in enumerate(group_order):
            da = jnp.where(step == index, group[0], da)
            db = jnp.where(step == index, group[1], db)
        for other in range(2):
            part_logits = logits[:, other * cap:(other + 1) * cap]
            tag = tags[device_at(da, db, other)] - first_column
            peak = jnp.max(part_logits, axis=0, keepdims=True)
            shifted = part_logits - peak
            exponent = jnp.exp(shifted)
            total = jnp.sum(exponent, axis=0, keepdims=True)
            spread = jnp.sum(exponent * shifted, axis=0, keepdims=True)
            column = lax.broadcasted_iota(jnp.int32, part_logits.shape, 0)
            picked = jnp.sum(jnp.where(column == tag, part_logits, 0.0), axis=0, keepdims=True)
            own_stats[step, other] = jnp.concatenate([peak, total, spread, picked] * 2, axis=0)

        for index, group in enumerate(group_order):
            @pl.when(step == index)
            def _():
                for other in range(2):
                    if index == 0 and other == 0:
                        stats_in[me] = own_stats[0, 0]
                    else:
                        stat_copy(group, other).start()
        return carry

    lax.fori_loop(0, len(group_order), one_group, 0)

    pltpu.make_async_copy(stats_in.at[pl.ds(0, members - 1)], stats_in.at[pl.ds(0, members - 1)], stat_recv).wait()

    peak = stats_in[0]
    for index in range(1, members):
        peak = jnp.maximum(peak, stats_in[index])
    peak = peak[0:1]
    row_total = jnp.zeros((1, cap), f32)
    spread = jnp.zeros((1, cap), f32)
    picked = jnp.zeros((1, cap), f32)
    for index in range(members):
        tile = stats_in[index]
        below = tile[0:1] - peak
        factor = jnp.exp(below)
        row_total = row_total + tile[1:2] * factor
        spread = spread + factor * (tile[2:3] + below * tile[1:2])
        picked = picked + tile[3:4]
    log_total = jnp.log(row_total)
    logprob = jnp.broadcast_to(picked - peak - log_total, (seq_count, cap))
    entropy = jnp.broadcast_to(log_total - spread / row_total, (seq_count, cap))

    request = lax.broadcasted_iota(jnp.int32, (seq_count, cap), 0)
    lane = lax.broadcasted_iota(jnp.int32, (seq_count, cap), 1)
    offset = jnp.zeros((seq_count, cap), jnp.int32)
    length = jnp.zeros((seq_count, cap), jnp.int32)
    for seq in range(seq_count):
        offset = jnp.where(request == seq, offsets[seq], offset)
        length = jnp.where(request == seq, lens[seq], length)
    bit = 1
    while bit < cap:
        moved = (offset & bit) != 0
        logprob = jnp.where(moved, pltpu.roll(logprob, cap - bit, 1), logprob)
        entropy = jnp.where(moved, pltpu.roll(entropy, cap - bit, 1), entropy)
        bit *= 2
    logprob = jnp.where(lane < length, logprob, 0.0)
    entropy = jnp.where(lane < length, entropy, 0.0)
    both = logprob + pltpu.roll(entropy, seq_len, 1)
    half = seq_count // 2
    fin[me, req] = both[:half] + pltpu.roll(both[half:], cap // 2, 1)

    def z_copy(step):
        return pltpu.make_async_remote_copy(
            src_ref=fin.at[me, req], dst_ref=fin.at[me, req], send_sem=z_send.at[step - 1], recv_sem=z_recv,
            device_id=(lax.rem(req + step, side), me), device_id_type=mesh_ids)

    for step in range(1, side):
        z_copy(step).start()
    pltpu.make_async_copy(fin.at[me, pl.ds(0, side - 1)], fin.at[me, pl.ds(0, side - 1)], z_recv).wait()

    def fin_copy(step):
        return pltpu.make_async_remote_copy(
            src_ref=fin.at[me], dst_ref=fin.at[me], send_sem=fin_send, recv_sem=fin_recv,
            device_id=(req, lax.rem(me + step, members)), device_id_type=mesh_ids)

    def send_fin(step, carry):
        fin_copy(step).start()
        return carry

    lax.fori_loop(1, members, send_fin, 0)
    pltpu.make_async_copy(fin.at[pl.ds(0, members - 1)], fin.at[pl.ds(0, members - 1)], fin_recv).wait()

    for seq in range(seq_count):
        wanted = slots[seq]
        owner = lax.div(wanted, seq_count)
        inside = lax.rem(wanted, seq_count)
        tile = fin[lax.rem(owner, members), lax.div(owner, members)]
        turned = pltpu.roll(tile, cap // 2, 1)
        tile = jnp.where(inside >= half, turned, tile)
        level = lax.rem(inside, half)
        row = lax.broadcasted_iota(jnp.int32, (half, cap), 0)
        gathered[pl.ds(seq, 1), :] = jnp.sum(jnp.where(row == level, tile, 0.0), axis=0, keepdims=True)
    out_logprob[...] = gathered[:, 0:seq_len]
    out_entropy[...] = gathered[:, seq_len:2 * seq_len]

    def drain(index, carry):
        here = rows.at[0, pl.ds(0, piece_rows), :]
        pltpu.make_async_copy(here, here, send_sem.at[index]).wait()
        return carry

    lax.fori_loop(0, send_count, drain, 0)
    pltpu.make_async_copy(tags.at[pl.ds(0, members - 1)], tags.at[pl.ds(0, members - 1)], tag_send).wait()

    def drain_stats(index, carry):
        pltpu.make_async_copy(stats_in.at[0], stats_in.at[0], stat_send.at[index]).wait()
        return carry

    lax.fori_loop(1, 2 * len(group_order), drain_stats, 0)
    for step in range(1, side):
        z_copy(step).wait_send()
    pltpu.make_async_copy(fin.at[pl.ds(0, members - 1)], fin.at[pl.ds(0, members - 1)], fin_send).wait()


def local(hidden_states, norm_gain, head_weight, targets, lengths, slot_of):
    held, depth = hidden_states.shape
    seq_count = lengths.shape[0]
    seq_len = held // seq_count
    columns = head_weight.shape[1]
    groups = side * side
    members = 2 * groups
    vmem = pl.BlockSpec(memory_space=pltpu.VMEM)
    smem = pl.BlockSpec(memory_space=pltpu.SMEM)
    dma = pltpu.SemaphoreType.DMA
    out = jax.ShapeDtypeStruct((seq_count, seq_len), f32)
    return pl.pallas_call(
        kernel,
        out_shape=(out, out),
        in_specs=[smem, smem, vmem, vmem, vmem, pl.BlockSpec(memory_space=pl.ANY)],
        out_specs=(vmem, vmem),
        scratch_shapes=[
            pltpu.VMEM((depth, columns), jnp.bfloat16),
            pltpu.VMEM((columns, depth), jnp.bfloat16),
            pltpu.VMEM((groups, 2 * cap, depth), jnp.bfloat16),
            pltpu.VMEM((members, 1, cap), jnp.int32),
            pltpu.VMEM((1, 1, cap), jnp.int32),
            pltpu.VMEM((groups, 2, 8, cap), f32),
            pltpu.VMEM((members, 8, cap), f32),
            pltpu.VMEM((members, side, seq_count // 2, cap), f32),
            pltpu.VMEM((seq_count, cap), f32),
            dma,
            dma((send_count,)),
            dma((groups * pieces,)),
            dma((groups * pieces,)),
            dma, dma,
            dma((members,)),
            dma,
            dma((side - 1,)),
            dma, dma, dma,
        ],
        compiler_params=pltpu.CompilerParams(collective_id=0, has_side_effects=True, vmem_limit_bytes=60 << 20),
        name="head_stats",
    )(lengths, slot_of, hidden_states, norm_gain.reshape(1, depth), targets.reshape(1, held), head_weight)


def solution(mesh):
    rows = jax.sharding.PartitionSpec(("req", "vocab"), None)
    flat = jax.sharding.PartitionSpec(("req", "vocab"))
    in_specs = (rows, jax.sharding.PartitionSpec(), jax.sharding.PartitionSpec(None, "vocab"), flat, flat, flat)
    return jax.shard_map(local, mesh=mesh, in_specs=in_specs, out_specs=(rows, rows), check_vma=False)
```

time: 518 us -> 95.7 us (0.18)
  blocking collectives: 320 us -> 0 us
  waiting for transfers between devices: 101 us -> 0 us
  Pallas kernels: 0 us -> 85.9 us
  matrix products: 61.4 us -> 0 us
  between operations: 14.8 us -> 0.64 us
  other arithmetic: 12.7 us -> 0 us
    unnamed x1 -> x0, blocking collectives: 127 us -> none
    pmax x1 -> x0, blocking collectives: 124 us -> none  [local(): peak_all = lax.pmax(group_stats[0], 'vocab')]
    psum x1 -> x0, waiting for transfers between devices: 101 us -> none  [local(): summed = lax.psum((scaled_total, scaled_spread, picked_all), 'vocab')]
    pallas_call x0 -> x1, Pallas kernels: none -> 85.9 us  [local(): pl.pallas_call(kernel, out_shape=(out, out), in_specs=[smem, smem, vmem,...]
    all_gather x2 -> x0, blocking collectives: 68.6 us -> none  [the longest x1 34.7 us: local(): lax.all_gather(slot_logprob, ('req', 'vocab'), axis=0, tiled=True)]
    dot_general x12 -> x0, matrix products: 61.4 us -> none  [piece_stats(): jnp.dot(piece_rows, head_weight, preferred_element_type=jnp.float32)]
    reduce_sum x13 -> x0, other arithmetic: 8.79 us -> none  [the longest x12 7.41 us: piece_stats(): spread = jnp.sum(exponent * shifted, axis=1)]
    unnamed x11 -> x3, local copies, waits for them, and re-layouts: 0.89 us -> 8.92 us
  transfers between devices with their start and end apart: 2 -> 0, of which waited for: 1 -> 0; matrix products, arithmetic and copies ran while one was open for 0% -> 0% of each run, Pallas kernels for 0% -> 0%
where the time goes in v1:
time: 95.7 us; the launch traced here: 95.4 us
  Pallas kernels  85.9 us (90%)
  local copies, waits for them, and re-layouts  8.92 us (9%)
    pallas_call x1, Pallas kernels, local(): pl.pallas_call(kernel, out_shape=(out, out), in_specs=[smem, smem, vmem,...  85.9 us
    unnamed x3, local copies, waits for them, and re-layouts  8.92 us

profile of v1, /device:TPU:1, one launch (start us, length us, event | category | flops | bytes accessed | tf_op | source)
XLA Modules:
  0.0 95.4 jit_solution(16717562171897695594)
XLA Ops:
  0.6 6.4 %copy.8.weight_hbm = bf16[2048,1000]{1,0:T(8,128)(2,1)} copy(bf16[2048,1000]{0,1:T(8,128)(2,1)} %param.8) | data formatting | bytes 8192000 | tf_op args[2]
  7.0 85.9 %head_stats.1 = (f32[8,24]{1,0:T(8,128)}, f32[8,24]{1,0:T(8,128)}) custom-call(s32[8]{0:T(128)} %lens.1, s32[8]{0:T(128)} %slots.1, bf16[192,2048]{1,0:T(8,128)(2,1)} %hidden.1, f32[1,2048]{1,0:T(1,128)} %bitcast.2, s32[1,192]{1,0:T(1,128)} %bitcast.3, bf16[2048,1000]{1,0:T(8,128)(2,1)} %copy.8.weight_hbm), custom_call_target="tpu_custom_call" | custom-call | tf_op jit(solution)/shard_map/head_stats/pallas_call | solution.py:340
  92.9 1.3 %copy.11 = f32[8,24]{1,0:T(8,128)} copy(f32[8,24]{1,0:T(8,128)} %get-tuple-element.4) | data formatting | bytes 1536
  94.2 1.3 %copy.12 = f32[8,24]{1,0:T(8,128)} copy(f32[8,24]{1,0:T(8,128)} %get-tuple-element.5) | data formatting | bytes 1536

commit v2 on v1

--- a/solution.py
+++ b/solution.py
@@ -62,7 +62,7 @@
 
 
 def kernel(lens, slots, hidden, gain, targets, weight_hbm, out_logprob, out_entropy,
-           weight, weight_t, rows, tags, tag_out, own_stats, stats_in, fin, gathered,
+           weight_t, rows, tags, tag_out, own_stats, stats_in, fin, gathered,
            weight_sem, send_sem, arrive_sem, partner_sem, tag_send, tag_recv,
            stat_send, stat_recv, z_send, z_recv, fin_send, fin_recv):
     req = lax.axis_index("req")
@@ -71,7 +71,7 @@
     chip_x = lax.rem(me // 2, side)
     chip_y = me // (2 * side)
     members = 2 * side * side
-    columns = weight.shape[1]
+    columns, depth = weight_t.shape
 
     def device_at(da, db, other):
         x = lax.rem(chip_x + da * (1 - core) + db * core, side)
@@ -89,7 +89,7 @@
     for step in range(1, side):
         pl.semaphore_signal(barrier, inc=1, device_id=(lax.rem(req + step, side), me), device_id_type=mesh_ids)
 
-    weight_copy = pltpu.make_async_copy(weight_hbm, weight, weight_sem)
+    weight_copy = pltpu.make_async_copy(weight_hbm, weight_t, weight_sem)
     weight_copy.start()
 
     seq_count = lens.shape[0]
@@ -170,16 +170,6 @@
     lax.fori_loop(1, members, send_tag, 0)
 
     weight_copy.wait()
-    depth = weight.shape[0]
-    chunk = 256
-
-    def turn(step, carry):
-        start = pl.multiple_of(step * chunk, chunk)
-        weight_t[:, pl.ds(start, chunk)] = weight[pl.ds(start, chunk), :].T
-        return carry
-
-    lax.fori_loop(0, depth // chunk, turn, 0)
-
     pltpu.make_async_copy(tags.at[pl.ds(0, members - 1)], tags.at[pl.ds(0, members - 1)], tag_recv).wait()
 
     def stat_copy(group, other):
@@ -343,7 +333,6 @@
         in_specs=[smem, smem, vmem, vmem, vmem, pl.BlockSpec(memory_space=pl.ANY)],
         out_specs=(vmem, vmem),
         scratch_shapes=[
-            pltpu.VMEM((depth, columns), jnp.bfloat16),
             pltpu.VMEM((columns, depth), jnp.bfloat16),
             pltpu.VMEM((groups, 2 * cap, depth), jnp.bfloat16),
             pltpu.VMEM((members, 1, cap), jnp.int32),
@@ -364,7 +353,7 @@
         ],
         compiler_params=pltpu.CompilerParams(collective_id=0, has_side_effects=True, vmem_limit_bytes=60 << 20),
         name="head_stats",
-    )(lengths, slot_of, hidden_states, norm_gain.reshape(1, depth), targets.reshape(1, held), head_weight)
+    )(lengths, slot_of, hidden_states, norm_gain.reshape(1, depth), targets.reshape(1, held), head_weight.T)
 
 
 def solution(mesh):

time: 95.7 us -> 89.2 us (0.932)
  local copies, waits for them, and re-layouts: 8.92 us -> 2.53 us
    unnamed x3 -> x2, local copies, waits for them, and re-layouts: 8.92 us -> 2.53 us
where the time goes in v2:
time: 89.2 us; the launch traced here: 89 us
  Pallas kernels  85.9 us (96%)
  local copies, waits for them, and re-layouts  2.53 us (3%)
    pallas_call x1, Pallas kernels, local(): pl.pallas_call(kernel, out_shape=(out, out), in_specs=[smem, smem, vmem,...  85.9 us
    unnamed x2, local copies, waits for them, and re-layouts  2.53 us

profile of v2, /device:TPU:1, one launch (start us, length us, event | category | flops | bytes accessed | tf_op | source)
XLA Modules:
  0.0 89.0 jit_solution(17746355495228573583)
XLA Ops:
  0.6 85.9 %head_stats.1 = (f32[8,24]{1,0:T(8,128)}, f32[8,24]{1,0:T(8,128)}) custom-call(s32[8]{0:T(128)} %lens.1, s32[8]{0:T(128)} %slots.1, bf16[192,2048]{1,0:T(8,128)(2,1)} %hidden.1, f32[1,2048]{1,0:T(1,128)} %bitcast.4, s32[1,192]{1,0:T(1,128)} %bitcast.5, bf16[1000,2048]{1,0:T(8,128)(2,1)} %bitcast.3), custom_call_target="tpu_custom_call" | custom-call | tf_op jit(solution)/shard_map/head_stats/pallas_call | solution.py:330
  86.5 1.3 %copy.10 = f32[8,24]{1,0:T(8,128)} copy(f32[8,24]{1,0:T(8,128)} %get-tuple-element.4) | data formatting | bytes 1536
  87.8 1.3 %copy.11 = f32[8,24]{1,0:T(8,128)} copy(f32[8,24]{1,0:T(8,128)} %get-tuple-element.5) | data formatting | bytes 1536

commit v3 on v2

--- a/solution.py
+++ b/solution.py
@@ -52,6 +52,19 @@
     return taken
 
 
+def tag_part(group, link):
+    if link == "partner":
+        return 0
+    carried = [part for part in range(pieces) if link in onward(*group, part)]
+    return carried[0] if carried else None
+
+
+tag_plan = {}
+for tag_group in group_order:
+    for tag_link in ["partner"] + list(range(4)):
+        if tag_part(tag_group, tag_link) == 0:
+            tag_plan[(tag_group, tag_link)] = len(tag_plan)
+
 send_count = 0
 send_plan = {}
 for arrival_group in group_order:
@@ -61,10 +74,10 @@
             send_count += 1
 
 
-def kernel(lens, slots, hidden, gain, targets, weight_hbm, out_logprob, out_entropy,
-           weight_t, rows, tags, tag_out, own_stats, stats_in, fin, gathered,
+def kernel(lens, slots, hidden, gain, targets, weight_hbm, out,
+           weight_t, rows, tags, own_stats, stats_in, fin, gathered,
            weight_sem, send_sem, arrive_sem, partner_sem, tag_send, tag_recv,
-           stat_send, stat_recv, z_send, z_recv, fin_send, fin_recv):
+           stat_send, stat_recv, token, fin_send, fin_recv):
     req = lax.axis_index("req")
     me = lax.axis_index("vocab")
     core = lax.rem(me, 2)
@@ -81,11 +94,9 @@
 
     barrier = pltpu.get_barrier_semaphore()
 
-    def greet(step, carry):
-        pl.semaphore_signal(barrier, inc=1, device_id=(req, lax.rem(me + step, members)), device_id_type=mesh_ids)
-        return carry
-
-    lax.fori_loop(1, members, greet, 0)
+    neighbours = [(1, 0, False), (3, 0, False), (0, 1, False), (0, 3, False), (0, 0, True)]
+    for neighbour in neighbours:
+        pl.semaphore_signal(barrier, inc=1, device_id=(req, device_at(*neighbour)), device_id_type=mesh_ids)
     for step in range(1, side):
         pl.semaphore_signal(barrier, inc=1, device_id=(lax.rem(req + step, side), me), device_id_type=mesh_ids)
 
@@ -122,10 +133,9 @@
     digits = digits.astype(f32).astype(jnp.bfloat16)
     tag_pair = jnp.dot(digits, pick_t, preferred_element_type=f32)
     tag_own = (tag_pair[0:1] * 256.0 + tag_pair[1:2]).astype(jnp.int32)
-    tag_out[0] = tag_own
-    tags[me] = tag_own
-
-    pl.semaphore_wait(barrier, members - 1 + side - 1)
+    tags[0] = tag_own
+
+    pl.semaphore_wait(barrier, len(neighbours) + side - 1)
 
     def piece_copy(group, part, link):
         da, db = group
@@ -150,27 +160,35 @@
         here = rows.at[slot, pl.ds(part * piece_rows, piece_rows), :]
         return pltpu.make_async_copy(here, here, arrive_sem.at[slot * pieces + part])
 
+    def tag_copy(group, link):
+        da, db = group
+        if link == "partner":
+            landing = slot_at[(db, da)] * 2 + 1
+            target = device_at(0, 0, True)
+        else:
+            ma, mb = links[link]
+            landing = slot_at[((da - ma) % side, (db - mb) % side)] * 2
+            target = device_at(ma, mb, False)
+        return pltpu.make_async_remote_copy(
+            src_ref=tags.at[slot_at[group] * 2], dst_ref=tags.at[landing],
+            send_sem=tag_send.at[tag_plan[(group, link)]], recv_sem=tag_recv.at[landing],
+            device_id=(req, target), device_id_type=mesh_ids)
+
+    def tag_here(landing):
+        return pltpu.make_async_copy(tags.at[landing], tags.at[landing], tag_recv.at[landing])
+
     def send_onward(da, db, part):
         for link in onward(da, db, part):
             piece_copy((da, db), part, link).start()
         piece_copy((da, db), part, "partner").start()
+        for link in ["partner"] + list(range(4)):
+            if part == 0 and (((da, db), link) in tag_plan):
+                tag_copy((da, db), link).start()
 
     for part in range(pieces):
         send_onward(0, 0, part)
 
-    def tag_copy(step):
-        return pltpu.make_async_remote_copy(
-            src_ref=tag_out.at[0], dst_ref=tags.at[me], send_sem=tag_send, recv_sem=tag_recv,
-            device_id=(req, lax.rem(me + step, members)), device_id_type=mesh_ids)
-
-    def send_tag(step, carry):
-        tag_copy(step).start()
-        return carry
-
-    lax.fori_loop(1, members, send_tag, 0)
-
     weight_copy.wait()
-    pltpu.make_async_copy(tags.at[pl.ds(0, members - 1)], tags.at[pl.ds(0, members - 1)], tag_recv).wait()
 
     def stat_copy(group, other):
         owner = device_at(group[0], group[1], other)
@@ -189,21 +207,24 @@
                 def _():
                     for da, db, part in arrivals[index]:
                         arrived(slot_at[(da, db)], part).wait()
+                        if part == 0:
+                            tag_here(slot_at[(da, db)] * 2).wait()
                         send_onward(da, db, part)
 
         for part in range(pieces):
             there = rows.at[step, pl.ds(cap + part * piece_rows, piece_rows), :]
             pltpu.make_async_copy(there, there, partner_sem.at[step * pieces + part]).wait()
+        tag_here(step * 2 + 1).wait()
+
+        @pl.when(step == len(group_order) - 1)
+        def _():
+            for ahead in range(1, side):
+                pl.semaphore_signal(token, inc=1, device_id=(lax.rem(req + ahead, side), me), device_id_type=mesh_ids)
 
         logits = lax.dot_general(weight_t[...], rows[step], (((1,), (1,)), ((), ())), preferred_element_type=f32)
-        da = jnp.int32(0)
-        db = jnp.int32(0)
-        for index, group in enumerate(group_order):
-            da = jnp.where(step == index, group[0], da)
-            db = jnp.where(step == index, group[1], db)
         for other in range(2):
             part_logits = logits[:, other * cap:(other + 1) * cap]
-            tag = tags[device_at(da, db, other)] - first_column
+            tag = tags[step * 2 + other] - first_column
             peak = jnp.max(part_logits, axis=0, keepdims=True)
             shifted = part_logits - peak
             exponent = jnp.exp(shifted)
@@ -262,41 +283,37 @@
     entropy = jnp.where(lane < length, entropy, 0.0)
     both = logprob + pltpu.roll(entropy, seq_len, 1)
     half = seq_count // 2
-    fin[me, req] = both[:half] + pltpu.roll(both[half:], cap // 2, 1)
-
-    def z_copy(step):
+    fin[req * members + me] = both[:half] + pltpu.roll(both[half:], cap // 2, 1)
+
+    pl.semaphore_wait(token, side - 1)
+    mine = req * members + me
+
+    def fin_copy(step):
+        other = lax.rem(mine + step, members * side)
         return pltpu.make_async_remote_copy(
-            src_ref=fin.at[me, req], dst_ref=fin.at[me, req], send_sem=z_send.at[step - 1], recv_sem=z_recv,
-            device_id=(lax.rem(req + step, side), me), device_id_type=mesh_ids)
-
-    for step in range(1, side):
-        z_copy(step).start()
-    pltpu.make_async_copy(fin.at[me, pl.ds(0, side - 1)], fin.at[me, pl.ds(0, side - 1)], z_recv).wait()
-
-    def fin_copy(step):
-        return pltpu.make_async_remote_copy(
-            src_ref=fin.at[me], dst_ref=fin.at[me], send_sem=fin_send, recv_sem=fin_recv,
-            device_id=(req, lax.rem(me + step, members)), device_id_type=mesh_ids)
+            src_ref=fin.at[mine], dst_ref=fin.at[mine], send_sem=fin_send, recv_sem=fin_recv,
+            device_id=(other // members, lax.rem(other, members)), device_id_type=mesh_ids)
 
     def send_fin(step, carry):
         fin_copy(step).start()
         return carry
 
-    lax.fori_loop(1, members, send_fin, 0)
-    pltpu.make_async_copy(fin.at[pl.ds(0, members - 1)], fin.at[pl.ds(0, members - 1)], fin_recv).wait()
+    lax.fori_loop(1, members * side, send_fin, 0)
+    others = fin.at[pl.ds(0, members * side - 1)]
+    pltpu.make_async_copy(others, others, fin_recv).wait()
 
     for seq in range(seq_count):
         wanted = slots[seq]
         owner = lax.div(wanted, seq_count)
         inside = lax.rem(wanted, seq_count)
-        tile = fin[lax.rem(owner, members), lax.div(owner, members)]
+        tile = fin[owner]
         turned = pltpu.roll(tile, cap // 2, 1)
         tile = jnp.where(inside >= half, turned, tile)
         level = lax.rem(inside, half)
         row = lax.broadcasted_iota(jnp.int32, (half, cap), 0)
         gathered[pl.ds(seq, 1), :] = jnp.sum(jnp.where(row == level, tile, 0.0), axis=0, keepdims=True)
-    out_logprob[...] = gathered[:, 0:seq_len]
-    out_entropy[...] = gathered[:, seq_len:2 * seq_len]
+    out[0] = gathered[:, 0:seq_len]
+    out[1] = gathered[:, seq_len:2 * seq_len]
 
     def drain(index, carry):
         here = rows.at[0, pl.ds(0, piece_rows), :]
@@ -304,16 +321,18 @@
         return carry
 
     lax.fori_loop(0, send_count, drain, 0)
-    pltpu.make_async_copy(tags.at[pl.ds(0, members - 1)], tags.at[pl.ds(0, members - 1)], tag_send).wait()
+    def drain_tags(index, carry):
+        pltpu.make_async_copy(tags.at[0], tags.at[0], tag_send.at[index]).wait()
+        return carry
+
+    lax.fori_loop(0, len(tag_plan), drain_tags, 0)
 
     def drain_stats(index, carry):
         pltpu.make_async_copy(stats_in.at[0], stats_in.at[0], stat_send.at[index]).wait()
         return carry
 
     lax.fori_loop(1, 2 * len(group_order), drain_stats, 0)
-    for step in range(1, side):
-        z_copy(step).wait_send()
-    pltpu.make_async_copy(fin.at[pl.ds(0, members - 1)], fin.at[pl.ds(0, members - 1)], fin_send).wait()
+    pltpu.make_async_copy(others, others, fin_send).wait()
 
 
 def local(hidden_states, norm_gain, head_weight, targets, lengths, slot_of):
@@ -326,34 +345,35 @@
     vmem = pl.BlockSpec(memory_space=pltpu.VMEM)
     smem = pl.BlockSpec(memory_space=pltpu.SMEM)
     dma = pltpu.SemaphoreType.DMA
-    out = jax.ShapeDtypeStruct((seq_count, seq_len), f32)
-    return pl.pallas_call(
+    out = jax.ShapeDtypeStruct((2, seq_count, seq_len), f32)
+    both = pl.pallas_call(
         kernel,
-        out_shape=(out, out),
+        out_shape=out,
         in_specs=[smem, smem, vmem, vmem, vmem, pl.BlockSpec(memory_space=pl.ANY)],
-        out_specs=(vmem, vmem),
+        out_specs=vmem,
         scratch_shapes=[
             pltpu.VMEM((columns, depth), jnp.bfloat16),
             pltpu.VMEM((groups, 2 * cap, depth), jnp.bfloat16),
             pltpu.VMEM((members, 1, cap), jnp.int32),
-            pltpu.VMEM((1, 1, cap), jnp.int32),
             pltpu.VMEM((groups, 2, 8, cap), f32),
             pltpu.VMEM((members, 8, cap), f32),
-            pltpu.VMEM((members, side, seq_count // 2, cap), f32),
+            pltpu.VMEM((members * side, seq_count // 2, cap), f32),
             pltpu.VMEM((seq_count, cap), f32),
             dma,
             dma((send_count,)),
             dma((groups * pieces,)),
             dma((groups * pieces,)),
-            dma, dma,
+            dma((len(tag_plan),)),
+            dma((members,)),
             dma((members,)),
             dma,
-            dma((side - 1,)),
-            dma, dma, dma,
+            pltpu.SemaphoreType.REGULAR,
+            dma, dma,
         ],
         compiler_params=pltpu.CompilerParams(collective_id=0, has_side_effects=True, vmem_limit_bytes=60 << 20),
         name="head_stats",
     )(lengths, slot_of, hidden_states, norm_gain.reshape(1, depth), targets.reshape(1, held), head_weight.T)
+    return (both[0], both[1])
 
 
 def solution(mesh):

time: 89.2 us -> 79.3 us (0.89)
  Pallas kernels: 85.9 us -> 77.3 us
  local copies, waits for them, and re-layouts: 2.53 us -> 1.28 us
    pallas_call x1, Pallas kernels: 85.9 us -> 77.3 us  [local(): pl.pallas_call(kernel, out_shape=out, in_specs=[smem, smem, vmem, vmem, v...]
    unnamed x2 -> x0, local copies, waits for them, and re-layouts: 2.53 us -> none
    squeeze x0 -> x1, local copies, waits for them, and re-layouts: none -> 1.28 us  [local(): return (both[0], both[1])]
where the time goes in v3:
time: 79.3 us; the launch traced here: 79.2 us
  Pallas kernels  77.3 us (97%)
  local copies, waits for them, and re-layouts  1.28 us (2%)
    pallas_call x1, Pallas kernels, local(): pl.pallas_call(kernel, out_shape=out, in_specs=[smem, smem, vmem, vmem, v...  77.3 us

profile of v3, /device:TPU:1, one launch (start us, length us, event | category | flops | bytes accessed | tf_op | source)
XLA Modules:
  0.0 79.2 jit_solution(15342837206237717519)
XLA Ops:
  0.6 77.3 %head_stats.1 = f32[2,8,24]{2,1,0:T(8,128)} custom-call(s32[8]{0:T(128)} %lens.1, s32[8]{0:T(128)} %slots.1, bf16[192,2048]{1,0:T(8,128)(2,1)} %hidden.1, f32[1,2048]{1,0:T(1,128)} %bitcast.8, s32[1,192]{1,0:T(1,128)} %bitcast.9, bf16[1000,2048]{1,0:T(8,128)(2,1)} %bitcast.7), custom_call_target="tpu_custom_call" | custom-call | tf_op jit(solution)/shard_map/head_stats/pallas_call | solution.py:349
  77.9 1.3 %slice_bitcast_fusion = (f32[8,24]{1,0:T(8,128)}, f32[8,24]{1,0:T(8,128)}) fusion(f32[2,8,24]{2,1,0:T(8,128)} %head_stats.1), kind=kLoop, calls=%fused_computation | loop fusion | bytes 3072 | tf_op jit(solution)/shard_map/squeeze | solution.py:376

commit v4 on v3

v4 whole, which is shorter than its diff:
```python
import jax
import jax.numpy as jnp
from jax import lax
from jax.experimental import pallas as pl
from jax.experimental.pallas import tpu as pltpu

eps_norm = 1e-05
side = 4
cap = 128
pieces = 4
piece_rows = cap // pieces
group_count = 2 * side
mesh_ids = pl.DeviceIdType.MESH
f32 = jnp.float32

sub_rows = (32, 32, 16, 32, 64, 32)
part_subs = ((0, 1, 2, 3), (4, 5))
rest_part = 1
steps = [
    ([], 0, 0),
    ([('W', 0, 0), ('R', 1, 0, 0), ('R', 0, 3, 0), ('R', 0, 1, 0), ('W', 0, 1), ('R', 0, 3, 2), ('R', 0, 1, 2), ('R', 1, 0, 2), ('W', 0, 2), ('W', 3, 0), ('W', 1, 0), ('R', 1, 0, 1), ('R', 0, 3, 1), ('R', 0, 1, 1), ('W', 0, 3), ('W', 3, 1), ('W', 1, 1), ('R', 0, 3, 3), ('R', 0, 1, 3), ('R', 1, 0, 3), ('W', 3, 2), ('W', 1, 2)], 0, 1),
    ([], 0, 3),
    ([('R', 1, 3, 0), ('R', 1, 1, 0), ('R', 1, 3, 2), ('W', 2, 0), ('W', 1, 3), ('W', 0, 4)], 0, 4),
    ([('R', 0, 2, 0), ('R', 1, 1, 2), ('R', 1, 1, 1), ('W', 3, 3), ('W', 2, 1), ('W', 0, 5), ('W', 2, 2), ('R', 0, 2, 2), ('R', 0, 2, 1), ('R', 1, 3, 3), ('W', 2, 3)], 1, 0),
    ([], 1, 1),
    ([], 1, 3),
    ([], 1, 4),
    ([('R', 1, 3, 1), ('R', 1, 1, 3), ('R', 0, 2, 3)], 0, 2),
    ([('W', 3, 4)], 0, 5),
    ([('R', 1, 2, 0), ('R', 1, 2, 1), ('R', 1, 2, 2), ('W', 1, 4)], 0, 7),
    ([('W', 3, 5), ('R', 1, 2, 3)], 1, 2),
    ([('W', 1, 5)], 1, 5),
    ([], 0, 6),
    ([], 1, 7),
    ([], 1, 6),
    ([('W', 2, 4), ('W', 2, 5), ('D', 0)], 2, 6),
    ([], 2, 2),
    ([], 2, 5),
    ([], 2, 7),
    ([], 2, 1),
    ([], 2, 3),
    ([], 2, 4),
    ([], 2, 0),
]
sub_start = [sum(sub_rows[:index]) for index in range(len(sub_rows))]
quarter = sum(sub_rows)
part_of_sub = {sub: part for part, subs in enumerate(part_subs) for sub in subs}
part_block = [sum(sub_rows[sub] for sub in subs) for subs in part_subs]


def row_links(p, dy, q):
    taken = []
    x_first = q < 2
    upward = q % 2 == 0
    if x_first:
        if (p, dy) == (0, 0):
            taken.append("x")
        if dy == 0:
            taken += ["up", "down"]
    else:
        if (p, dy) == (0, 0):
            taken += ["up", "down"]
        if p == 0:
            taken.append("x")
    if x_first or p == 0:
        if dy == 3 and upward:
            taken.append("up")
        if dy == 1 and not upward:
            taken.append("down")
    return taken


def row_landing(p, dy, link):
    if link == "x":
        return (1 - p, dy)
    if link == "partner":
        return (p, dy)
    return (p, (dy + (3 if link == "up" else 1)) % side)


def weight_links(d, sub):
    if d == 0:
        return ["up", "down"]
    if d == 3 and sub % 2 == 0:
        return ["up"]
    if d == 1 and sub % 2 == 1:
        return ["down"]
    return []


def weight_landing(d, link):
    return (d + (3 if link == "up" else 1)) % side


all_groups = [(p, dy) for p in range(2) for dy in range(side)]
row_plan = {}
tag_plan = {}
tag_first = {}
for plan_group in all_groups:
    for plan_link in ["partner", "x", "up", "down"]:
        for plan_piece in range(pieces):
            if plan_link == "partner" or plan_link in row_links(*plan_group, plan_piece):
                row_plan[(plan_group, plan_piece, plan_link)] = len(row_plan)
                landing_group = row_landing(*plan_group, plan_link)
                if plan_piece == 0:
                    tag_plan[(plan_group, plan_link)] = len(tag_plan)
weight_arrivals = [(d, sub) for d in range(side) for sub in range(len(sub_rows))]
weight_slot = {arrival: index for index, arrival in enumerate(weight_arrivals)}
rest_slot = len(weight_arrivals)
weight_plan = {}
for plan_arrival in weight_arrivals:
    for plan_link in weight_links(*plan_arrival):
        weight_plan[(plan_arrival, plan_link)] = len(weight_plan)
entry_plan = {sub: len(weight_plan) + sub for sub in range(len(sub_rows))}
rest_plan = len(weight_plan) + len(sub_rows)
weight_sends = rest_plan + 1
last_part = len(part_subs)
last_own_step = max(index for index, step_entry in enumerate(steps) if step_entry[1] == 0)


def kernel(lens, slots, hidden, gain, targets, weight_hbm, out, *scratch):
    weight_t, rows, tags, running, stats_in, fin, gathered = scratch[:7]
    pair_parts = scratch[7:7 + len(part_subs)]
    (weight_sem, row_send, row_recv, partner_recv, weight_send, weight_recv, tag_send, tag_recv,
     stat_send, stat_recv, token_x, token_z, fin_send, fin_recv) = scratch[7 + len(part_subs):]
    req = lax.axis_index("req")
    me = lax.axis_index("vocab")
    core = lax.rem(me, 2)
    chip_x = lax.rem(me // 2, side)
    chip_y = me // (2 * side)
    members = 2 * side * side
    columns, depth = weight_t.shape
    side_x = lax.rem(chip_x, 2)
    pair_x = side - 1 - chip_x

    def vocab_id(x, y, the_core):
        return (y * side + x) * 2 + the_core

    def group_owner(group, other):
        p, dy = group
        x = chip_x + p * (1 - 2 * side_x)
        return vocab_id(x, lax.rem(chip_y + dy, side), (1 - core) if other else core)

    def row_target(link):
        if link == "partner":
            return (req, vocab_id(chip_x, chip_y, 1 - core))
        if link == "x":
            return (req, group_owner((1, 0), False))
        return (req, group_owner((0, 1 if link == "up" else 3), False))

    def z_target(ahead):
        return (lax.rem(req + ahead, side), me)

    pair_target = (req, vocab_id(pair_x, chip_y, core))

    barrier = pltpu.get_barrier_semaphore()
    neighbours = [row_target(link) for link in ("partner", "x", "up", "down")] + [pair_target, z_target(1), z_target(3)]
    for neighbour in neighbours:
        pl.semaphore_signal(barrier, inc=1, device_id=neighbour, device_id_type=mesh_ids)

    weight_copy = pltpu.make_async_copy(weight_hbm, weight_t, weight_sem)
    weight_copy.start()

    seq_count = lens.shape[0]
    held = hidden.shape[0]
    seq_len = held // seq_count
    offsets = []
    total_length = jnp.int32(0)
    for seq in range(seq_count):
        offsets.append(total_length)
        total_length = total_length + lens[seq]

    def compact_place(slot_index):
        place = jnp.full(slot_index.shape, -1, jnp.int32)
        for seq in range(seq_count):
            ahead = slot_index - seq * seq_len
            place = jnp.where((ahead >= 0) & (ahead < lens[seq]), ahead + offsets[seq], place)
        return place

    place_row = compact_place(lax.broadcasted_iota(jnp.int32, (8, held), 1))[:1]
    pick = (lax.broadcasted_iota(jnp.int32, (cap, held), 0) == place_row).astype(f32).astype(jnp.bfloat16)
    live = jnp.dot(pick, hidden[...], preferred_element_type=f32)
    inverse_rms = lax.rsqrt(jnp.mean(live * live, axis=1, keepdims=True) + eps_norm)
    rows[0, 0:cap, :] = (live * inverse_rms * gain[...]).astype(jnp.bfloat16)

    place_col = compact_place(lax.broadcasted_iota(jnp.int32, (held, cap), 0))
    pick_t = (lax.broadcasted_iota(jnp.int32, (held, cap), 1) == place_col).astype(f32).astype(jnp.bfloat16)
    wide = targets[...]
    high = wide // 256
    digits = jnp.concatenate([high, wide - high * 256] + [jnp.zeros_like(wide)] * 14, axis=0)
    digits = digits.astype(f32).astype(jnp.bfloat16)
    tag_pair = jnp.dot(digits, pick_t, preferred_element_type=f32)
    tags[0] = (tag_pair[0:1] * 256.0 + tag_pair[1:2]).astype(jnp.int32)

    pl.semaphore_wait(barrier, len(neighbours))

    def part_rows(d, sub):
        part = part_of_sub[sub]
        start = d * part_block[part] + sub_start[sub] - sub_start[part_subs[part][0]]
        return pair_parts[part].at[pl.ds(start, sub_rows[sub]), :]

    def rest_rows():
        return pair_parts[rest_part].at[pl.ds(side * part_block[rest_part], columns - side * quarter), :]

    def entry_copy(sub):
        start = pl.multiple_of(req * quarter + sub_start[sub], 16)
        return pltpu.make_async_remote_copy(
            src_ref=weight_hbm.at[pl.ds(start, sub_rows[sub]), :], dst_ref=part_rows(0, sub),
            send_sem=weight_send.at[entry_plan[sub]], recv_sem=weight_recv.at[weight_slot[(0, sub)]],
            device_id=pair_target, device_id_type=mesh_ids)

    def rest_copy():
        return pltpu.make_async_remote_copy(
            src_ref=weight_hbm.at[pl.ds(side * quarter, columns - side * quarter), :], dst_ref=rest_rows(),
            send_sem=weight_send.at[rest_plan], recv_sem=weight_recv.at[rest_slot],
            device_id=pair_target, device_id_type=mesh_ids)

    def weight_relay(d, sub, link):
        landing = weight_landing(d, link)
        return pltpu.make_async_remote_copy(
            src_ref=part_rows(d, sub), dst_ref=part_rows(landing, sub),
            send_sem=weight_send.at[weight_plan[((d, sub), link)]], recv_sem=weight_recv.at[weight_slot[(landing, sub)]],
            device_id=z_target(1 if link == "up" else 3), device_id_type=mesh_ids)

    def row_index(group):
        return group[0] * side + group[1]

    def piece_copy(group, piece, link):
        landing = row_index(row_landing(*group, link))
        start = piece * piece_rows
        there = start + (cap if link == "partner" else 0)
        recv = (partner_recv if link == "partner" else row_recv).at[landing * pieces + piece]
        return pltpu.make_async_remote_copy(
            src_ref=rows.at[row_index(group), pl.ds(start, piece_rows), :],
            dst_ref=rows.at[landing, pl.ds(there, piece_rows), :],
            send_sem=row_send.at[row_plan[(group, piece, link)]], recv_sem=recv,
            device_id=row_target(link), device_id_type=mesh_ids)

    def tag_copy(group, link):
        landing = row_index(row_landing(*group, link)) * 2 + (1 if link == "partner" else 0)
        return pltpu.make_async_remote_copy(
            src_ref=tags.at[row_index(group) * 2], dst_ref=tags.at[landing],
            send_sem=tag_send.at[tag_plan[(group, link)]], recv_sem=tag_recv.at[landing],
            device_id=row_target(link), device_id_type=mesh_ids)

    def tag_here(landing):
        return pltpu.make_async_copy(tags.at[landing], tags.at[landing], tag_recv.at[landing])

    def send_onward(p, dy, piece):
        taken = row_links(p, dy, piece) + ["partner"]
        for link in taken:
            piece_copy((p, dy), piece, link).start()
        if piece == 0:
            for link in taken:
                tag_copy((p, dy), link).start()

    entry_copy(0).start()
    for piece in (0, 2, 1, 3):
        send_onward(0, 0, piece)
    for sub in range(1, len(sub_rows)):
        entry_copy(sub).start()
    rest_copy().start()

    weight_copy.wait()

    def arrival(event):
        if event[0] == "D":
            pltpu.make_async_copy(rest_rows(), rest_rows(), weight_recv.at[rest_slot]).wait()
        elif event[0] == "W":
            here = part_rows(event[1], event[2])
            pltpu.make_async_copy(here, here, weight_recv.at[weight_slot[event[1:]]]).wait()
            for link in weight_links(*event[1:]):
                weight_relay(event[1], event[2], link).start()
        else:
            group, piece = event[1:3], event[3]
            here = rows.at[row_index(group), pl.ds(piece * piece_rows, piece_rows), :]
            pltpu.make_async_copy(here, here, row_recv.at[row_index(group) * pieces + piece]).wait()
            if piece == 0:
                tag_here(row_index(group) * 2).wait()
            send_onward(*group, piece)

    my_place = (chip_y * 2 + side_x) * 2 + core

    def stat_copy(group, other):
        return pltpu.make_async_remote_copy(
            src_ref=running.at[row_index(group), other], dst_ref=stats_in.at[my_place],
            send_sem=stat_send.at[row_index(group) * 2 + other], recv_sem=stat_recv,
            device_id=(req, group_owner(group, other)), device_id_type=mesh_ids)

    own_first = me * columns
    pair_first = vocab_id(pair_x, chip_y, core) * columns
    own_blocks = [(0, columns, own_first)]

    def part_blocks(part):
        blocks = []
        for d in range(side):
            first = pair_first + lax.rem(req + d, side) * quarter + sub_start[part_subs[part][0]]
            blocks.append((d * part_block[part], part_block[part], first))
        if part == rest_part:
            blocks.append((side * part_block[part], columns - side * quarter, pair_first + side * quarter))
        return blocks

    def tile(group, weight_ref, blocks, fresh):
        logits = lax.dot_general(weight_ref[...], rows[group], (((1,), (1,)), ((), ())), preferred_element_type=f32)
        for other in range(2):
            piece = logits[:, other * cap:(other + 1) * cap]
            tag = tags[group * 2 + other]
            peak = jnp.max(piece, axis=0, keepdims=True)
            shifted = piece - peak
            exponent = jnp.exp(shifted)
            total = jnp.sum(exponent, axis=0, keepdims=True)
            spread = jnp.sum(exponent * shifted, axis=0, keepdims=True)
            picked = jnp.zeros((1, cap), f32)
            for start, size, first in blocks:
                column = lax.broadcasted_iota(jnp.int32, (size, cap), 0)
                block = piece[start:start + size]
                picked = picked + jnp.sum(jnp.where(column == tag - first, block, 0.0), axis=0, keepdims=True)
            if not fresh:
                before = running[group, other]
                joint = jnp.maximum(before[0:1], peak)
                drop_before = before[0:1] - joint
                drop = peak - joint
                factor_before = jnp.exp(drop_before)
                factor = jnp.exp(drop)
                spread = factor_before * (before[2:3] + drop_before * before[1:2]) + factor * (spread + drop * total)
                total = factor_before * before[1:2] + factor * total
                picked = picked + before[3:4]
                peak = joint
            running[group, other] = jnp.concatenate([peak, total, spread, picked] * 2, axis=0)

    def one_step(step, carry):
        for index, (events, kind, group) in enumerate(steps):
            if events:
                @pl.when(step == index)
                def _():
                    for event in events:
                        arrival(event)

        code = jnp.int32(0)
        for index, (events, kind, group) in enumerate(steps):
            code = jnp.where(step == index, kind * group_count + group, code)
        kind_now = code // group_count
        group_now = lax.rem(code, group_count)

        @pl.when(kind_now == 0)
        def _():
            for piece in range(pieces):
                there = rows.at[group_now, pl.ds(cap + piece * piece_rows, piece_rows), :]
                pltpu.make_async_copy(there, there, partner_recv.at[group_now * pieces + piece]).wait()
            landing = group_now * 2 + 1
            pltpu.make_async_copy(tags.at[landing], tags.at[landing], tag_recv.at[landing]).wait()
            tile(group_now, weight_t, own_blocks, True)

        for part in range(len(part_subs)):
            @pl.when(kind_now == part + 1)
            def _():
                tile(group_now, pair_parts[part], part_blocks(part), False)

        for index, (events, kind, group) in enumerate(steps):
            if kind == last_part:
                @pl.when(step == index)
                def _():
                    for other in range(2):
                        if group == 0 and other == 0:
                            stats_in[my_place] = running[0, 0]
                        else:
                            stat_copy(all_groups[group], other).start()

        @pl.when(step == last_own_step)
        def _():
            pl.semaphore_signal(token_x, inc=1, device_id=pair_target, device_id_type=mesh_ids)

        @pl.when(step == len(steps) - 3)
        def _():
            pl.semaphore_wait(token_x, 1)
            for ahead in range(1, side):
                pl.semaphore_signal(token_z, inc=1, device_id=z_target(ahead), device_id_type=mesh_ids)
        return carry

    lax.fori_loop(0, len(steps), one_step, 0)

    sources = 2 * group_count
    pltpu.make_async_copy(stats_in.at[pl.ds(0, sources - 1)], stats_in.at[pl.ds(0, sources - 1)], stat_recv).wait()

    peak = stats_in[0]
    for index in range(1, sources):
        peak = jnp.maximum(peak, stats_in[index])
    peak = peak[0:1]
    row_total = jnp.zeros((1, cap), f32)
    spread = jnp.zeros((1, cap), f32)
    picked = jnp.zeros((1, cap), f32)
    for index in range(sources):
        stat = stats_in[index]
        below = stat[0:1] - peak
        factor = jnp.exp(below)
        row_total = row_total + stat[1:2] * factor
        spread = spread + factor * (stat[2:3] + below * stat[1:2])
        picked = picked + stat[3:4]
    log_total = jnp.log(row_total)
    logprob = jnp.broadcast_to(picked - peak - log_total, (seq_count, cap))
    entropy = jnp.broadcast_to(log_total - spread / row_total, (seq_count, cap))

    request = lax.broadcasted_iota(jnp.int32, (seq_count, cap), 0)
    lane = lax.broadcasted_iota(jnp.int32, (seq_count, cap), 1)
    offset = jnp.zeros((seq_count, cap), jnp.int32)
    length = jnp.zeros((seq_count, cap), jnp.int32)
    for seq in range(seq_count):
        offset = jnp.where(request == seq, offsets[seq], offset)
        length = jnp.where(request == seq, lens[seq], length)
    bit = 1
    while bit < cap:
        moved = (offset & bit) != 0
        logprob = jnp.where(moved, pltpu.roll(logprob, cap - bit, 1), logprob)
        entropy = jnp.where(moved, pltpu.roll(entropy, cap - bit, 1), entropy)
        bit *= 2
    logprob = jnp.where(lane < length, logprob, 0.0)
    entropy = jnp.where(lane < length, entropy, 0.0)
    both = logprob + pltpu.roll(entropy, seq_len, 1)
    half = seq_count // 2
    mine = req * members + me
    fin[mine] = both[:half] + pltpu.roll(both[half:], cap // 2, 1)

    pl.semaphore_wait(token_z, side - 1)

    def fin_copy(step):
        other = lax.rem(mine + step, members * side)
        return pltpu.make_async_remote_copy(
            src_ref=fin.at[mine], dst_ref=fin.at[mine], send_sem=fin_send, recv_sem=fin_recv,
            device_id=(other // members, lax.rem(other, members)), device_id_type=mesh_ids)

    def send_fin(step, carry):
        fin_copy(step).start()
        return carry

    lax.fori_loop(1, members * side, send_fin, 0)
    others = fin.at[pl.ds(0, members * side - 1)]
    pltpu.make_async_copy(others, others, fin_recv).wait()

    for seq in range(seq_count):
        wanted = slots[seq]
        owner = lax.div(wanted, seq_count)
        inside = lax.rem(wanted, seq_count)
        found = fin[owner]
        turned = pltpu.roll(found, cap // 2, 1)
        found = jnp.where(inside >= half, turned, found)
        level = lax.rem(inside, half)
        row = lax.broadcasted_iota(jnp.int32, (half, cap), 0)
        gathered[pl.ds(seq, 1), :] = jnp.sum(jnp.where(row == level, found, 0.0), axis=0, keepdims=True)
    out[0] = gathered[:, 0:seq_len]
    out[1] = gathered[:, seq_len:2 * seq_len]

    def drain(index, carry):
        here = rows.at[0, pl.ds(0, piece_rows), :]
        pltpu.make_async_copy(here, here, row_send.at[index]).wait()
        return carry

    lax.fori_loop(0, len(row_plan), drain, 0)
    for (d, sub), link in weight_plan:
        weight_relay(d, sub, link).wait_send()
    for sub in range(len(sub_rows)):
        entry_copy(sub).wait_send()
    rest_copy().wait_send()

    def drain_tags(index, carry):
        pltpu.make_async_copy(tags.at[0], tags.at[0], tag_send.at[index]).wait()
        return carry

    lax.fori_loop(0, len(tag_plan), drain_tags, 0)

    def drain_stats(index, carry):
        pltpu.make_async_copy(stats_in.at[0], stats_in.at[0], stat_send.at[index]).wait()
        return carry

    lax.fori_loop(1, sources, drain_stats, 0)
    pltpu.make_async_copy(others, others, fin_send).wait()


def local(hidden_states, norm_gain, head_weight, targets, lengths, slot_of):
    held, depth = hidden_states.shape
    seq_count = lengths.shape[0]
    seq_len = held // seq_count
    columns = head_weight.shape[1]
    members = 2 * side * side
    vmem = pl.BlockSpec(memory_space=pltpu.VMEM)
    smem = pl.BlockSpec(memory_space=pltpu.SMEM)
    dma = pltpu.SemaphoreType.DMA
    regular = pltpu.SemaphoreType.REGULAR
    part_sizes = [side * block + (columns - side * quarter if part == rest_part else 0)
                  for part, block in enumerate(part_block)]
    out = jax.ShapeDtypeStruct((2, seq_count, seq_len), f32)
    both = pl.pallas_call(
        kernel,
        out_shape=out,
        in_specs=[smem, smem, vmem, vmem, vmem, pl.BlockSpec(memory_space=pl.ANY)],
        out_specs=vmem,
        scratch_shapes=[
            pltpu.VMEM((columns, depth), jnp.bfloat16),
            pltpu.VMEM((group_count, 2 * cap, depth), jnp.bfloat16),
            pltpu.VMEM((2 * group_count, 1, cap), jnp.int32),
            pltpu.VMEM((group_count, 2, 8, cap), f32),
            pltpu.VMEM((2 * group_count, 8, cap), f32),
            pltpu.VMEM((members * side, seq_count // 2, cap), f32),
            pltpu.VMEM((seq_count, cap), f32),
        ] + [pltpu.VMEM((size, depth), jnp.bfloat16) for size in part_sizes] + [
            dma,
            dma((len(row_plan),)),
            dma((group_count * pieces,)),
            dma((group_count * pieces,)),
            dma((weight_sends,)),
            dma((rest_slot + 1,)),
            dma((len(tag_plan),)),
            dma((2 * group_count,)),
            dma((2 * group_count,)),
            dma,
            regular,
            regular,
            dma,
            dma,
        ],
        compiler_params=pltpu.CompilerParams(collective_id=0, has_side_effects=True, vmem_limit_bytes=60 << 20),
        name="head_stats",
    )(lengths, slot_of, hidden_states, norm_gain.reshape(1, depth), targets.reshape(1, held), head_weight.T)
    return (both[0], both[1])


def solution(mesh):
    rows = jax.sharding.PartitionSpec(("req", "vocab"), None)
    flat = jax.sharding.PartitionSpec(("req", "vocab"))
    in_specs = (rows, jax.sharding.PartitionSpec(), jax.sharding.PartitionSpec(None, "vocab"), flat, flat, flat)
    return jax.shard_map(local, mesh=mesh, in_specs=in_specs, out_specs=(rows, rows), check_vma=False)
```

time: 79.3 us -> 74.4 us (0.938)
  Pallas kernels: 77.3 us -> 72.3 us
    pallas_call x1, Pallas kernels: 77.3 us -> 72.3 us  [local(): pl.pallas_call(kernel, out_shape=out, in_specs=[smem, smem, vmem, vmem, v...]
where the time goes in v4:
time: 74.4 us; the launch traced here: 74.3 us
  Pallas kernels  72.3 us (97%)
  local copies, waits for them, and re-layouts  1.28 us (2%)
    pallas_call x1, Pallas kernels, local(): pl.pallas_call(kernel, out_shape=out, in_specs=[smem, smem, vmem, vmem, v...  72.3 us

profile of v4, /device:TPU:1, one launch (start us, length us, event | category | flops | bytes accessed | tf_op | source)
XLA Modules:
  0.0 74.3 jit_solution(1694740195127903434)
XLA Ops:
  0.6 72.3 %head_stats.1 = f32[2,8,24]{2,1,0:T(8,128)} custom-call(s32[8]{0:T(128)} %lens.1, s32[8]{0:T(128)} %slots.1, bf16[192,2048]{1,0:T(8,128)(2,1)} %hidden.1, f32[1,2048]{1,0:T(1,128)} %bitcast.8, s32[1,192]{1,0:T(1,128)} %bitcast.9, bf16[1000,2048]{1,0:T(8,128)(2,1)} %bitcast.7), custom_call_target="tpu_custom_call" | custom-call | tf_op jit(solution)/shard_map/head_stats/pallas_call | solution.py:491
  73.0 1.3 %slice_bitcast_fusion = (f32[8,24]{1,0:T(8,128)}, f32[8,24]{1,0:T(8,128)}) fusion(f32[2,8,24]{2,1,0:T(8,128)} %head_stats.1), kind=kLoop, calls=%fused_computation | loop fusion | bytes 3072 | tf_op jit(solution)/shard_map/squeeze | solution.py:523

commit v5 on v4

--- a/solution.py
+++ b/solution.py
@@ -13,39 +13,55 @@
 mesh_ids = pl.DeviceIdType.MESH
 f32 = jnp.float32
 
-sub_rows = (32, 32, 16, 32, 64, 32)
-part_subs = ((0, 1, 2, 3), (4, 5))
-rest_part = 1
+sub_rows = (32, 32, 32, 32, 48, 32)
+rest_rows = (80, 88)
+entries = [("W", 0, 0), ("W", 0, 1), ("W", 0, 2), ("W", 0, 3), ("W", 0, 4), ("D", 0), ("W", 0, 5), ("D", 1)]
+parts = [[("W", 0, 0), ("W", 0, 1), ("W", 3, 0), ("W", 1, 0), ("W", 0, 2), ("W", 3, 1), ("W", 1, 1), ("W", 0, 3), ("W", 2, 0), ("W", 1, 2), ("W", 0, 4), ("W", 3, 2), ("W", 2, 1), ("W", 3, 3), ("W", 1, 3)], [("D", 0)], [("W", 3, 4), ("W", 1, 4), ("W", 0, 5), ("W", 2, 2), ("W", 2, 3), ("W", 1, 5), ("W", 2, 4), ("W", 3, 5), ("D", 1), ("W", 2, 5)]]
 steps = [
     ([], 0, 0),
-    ([('W', 0, 0), ('R', 1, 0, 0), ('R', 0, 3, 0), ('R', 0, 1, 0), ('W', 0, 1), ('R', 0, 3, 2), ('R', 0, 1, 2), ('R', 1, 0, 2), ('W', 0, 2), ('W', 3, 0), ('W', 1, 0), ('R', 1, 0, 1), ('R', 0, 3, 1), ('R', 0, 1, 1), ('W', 0, 3), ('W', 3, 1), ('W', 1, 1), ('R', 0, 3, 3), ('R', 0, 1, 3), ('R', 1, 0, 3), ('W', 3, 2), ('W', 1, 2)], 0, 1),
-    ([], 0, 3),
-    ([('R', 1, 3, 0), ('R', 1, 1, 0), ('R', 1, 3, 2), ('W', 2, 0), ('W', 1, 3), ('W', 0, 4)], 0, 4),
-    ([('R', 0, 2, 0), ('R', 1, 1, 2), ('R', 1, 1, 1), ('W', 3, 3), ('W', 2, 1), ('W', 0, 5), ('W', 2, 2), ('R', 0, 2, 2), ('R', 0, 2, 1), ('R', 1, 3, 3), ('W', 2, 3)], 1, 0),
+    ([("W", 0, 0), ("R", 1, 0, 0), ("R", 0, 3, 0), ("R", 0, 1, 0), ("W", 0, 1), ("R", 0, 3, 2), ("R", 0, 1, 2), ("R", 1, 0, 2), ("W", 3, 0), ("W", 1, 0), ("W", 0, 2), ("R", 1, 0, 1), ("R", 0, 3, 1), ("R", 0, 1, 1), ("W", 3, 1), ("W", 1, 1), ("W", 0, 3), ("R", 0, 3, 3), ("R", 0, 1, 3), ("R", 1, 0, 3)], 0, 1),
+    ([("W", 2, 0), ("W", 1, 2), ("R", 1, 3, 0), ("R", 1, 1, 0), ("R", 1, 3, 2)], 0, 3),
+    ([("W", 0, 4), ("W", 3, 2), ("W", 2, 1)], 0, 4),
+    ([("R", 0, 2, 0), ("R", 1, 1, 2), ("R", 1, 1, 1), ("W", 3, 3), ("W", 1, 3)], 1, 0),
     ([], 1, 1),
-    ([], 1, 3),
+    ([("R", 0, 2, 2), ("R", 0, 2, 1), ("R", 1, 3, 3)], 1, 3),
     ([], 1, 4),
-    ([('R', 1, 3, 1), ('R', 1, 1, 3), ('R', 0, 2, 3)], 0, 2),
-    ([('W', 3, 4)], 0, 5),
-    ([('R', 1, 2, 0), ('R', 1, 2, 1), ('R', 1, 2, 2), ('W', 1, 4)], 0, 7),
-    ([('W', 3, 5), ('R', 1, 2, 3)], 1, 2),
-    ([('W', 1, 5)], 1, 5),
-    ([], 0, 6),
-    ([], 1, 7),
-    ([], 1, 6),
-    ([('W', 2, 4), ('W', 2, 5), ('D', 0)], 2, 6),
-    ([], 2, 2),
-    ([], 2, 5),
-    ([], 2, 7),
-    ([], 2, 1),
+    ([("D", 0), ("R", 1, 3, 1), ("R", 1, 1, 3), ("R", 0, 2, 3)], 2, 0),
+    ([("W", 3, 4), ("W", 1, 4)], 2, 1),
     ([], 2, 3),
     ([], 2, 4),
-    ([], 2, 0),
+    ([], 0, 2),
+    ([("W", 0, 5), ("R", 1, 2, 0), ("R", 1, 2, 1), ("R", 1, 2, 2)], 0, 5),
+    ([("W", 2, 2), ("W", 2, 3)], 0, 7),
+    ([("R", 1, 2, 3)], 1, 2),
+    ([], 1, 5),
+    ([("W", 1, 5), ("W", 2, 4)], 0, 6),
+    ([], 1, 7),
+    ([("W", 3, 5)], 1, 6),
+    ([("D", 1)], 2, 2),
+    ([], 2, 5),
+    ([("W", 2, 5)], 2, 7),
+    ([], 2, 6),
+    ([], 3, 6),
+    ([], 3, 2),
+    ([], 3, 5),
+    ([], 3, 7),
+    ([], 3, 1),
+    ([], 3, 3),
+    ([], 3, 4),
+    ([], 3, 0),
 ]
 sub_start = [sum(sub_rows[:index]) for index in range(len(sub_rows))]
 quarter = sum(sub_rows)
-part_of_sub = {sub: part for part, subs in enumerate(part_subs) for sub in subs}
-part_block = [sum(sub_rows[sub] for sub in subs) for subs in part_subs]
+part_place = {}
+part_sizes = []
+for part_index, part_list in enumerate(parts):
+    filled = 0
+    for part_piece in part_list:
+        part_place[part_piece] = (part_index, filled)
+        filled += sub_rows[part_piece[2]] if part_piece[0] == "W" else rest_rows[part_piece[1]]
+    part_sizes.append(filled)
+rest_start = [side * quarter + sum(rest_rows[:index]) for index in range(len(rest_rows))]
 
 
 def row_links(p, dy, q):
@@ -106,23 +122,23 @@
                     tag_plan[(plan_group, plan_link)] = len(tag_plan)
 weight_arrivals = [(d, sub) for d in range(side) for sub in range(len(sub_rows))]
 weight_slot = {arrival: index for index, arrival in enumerate(weight_arrivals)}
-rest_slot = len(weight_arrivals)
+rest_slots = [len(weight_arrivals) + index for index in range(len(rest_rows))]
 weight_plan = {}
 for plan_arrival in weight_arrivals:
     for plan_link in weight_links(*plan_arrival):
         weight_plan[(plan_arrival, plan_link)] = len(weight_plan)
 entry_plan = {sub: len(weight_plan) + sub for sub in range(len(sub_rows))}
-rest_plan = len(weight_plan) + len(sub_rows)
-weight_sends = rest_plan + 1
-last_part = len(part_subs)
+rest_plan = [len(weight_plan) + len(sub_rows) + index for index in range(len(rest_rows))]
+weight_sends = rest_plan[-1] + 1
+last_part = len(parts)
 last_own_step = max(index for index, step_entry in enumerate(steps) if step_entry[1] == 0)
 
 
 def kernel(lens, slots, hidden, gain, targets, weight_hbm, out, *scratch):
     weight_t, rows, tags, running, stats_in, fin, gathered = scratch[:7]
-    pair_parts = scratch[7:7 + len(part_subs)]
+    pair_parts = scratch[7:7 + len(parts)]
     (weight_sem, row_send, row_recv, partner_recv, weight_send, weight_recv, tag_send, tag_recv,
-     stat_send, stat_recv, token_x, token_z, fin_send, fin_recv) = scratch[7 + len(part_subs):]
+     stat_send, stat_recv, token_x, token_z, fin_send, fin_recv) = scratch[7 + len(parts):]
     req = lax.axis_index("req")
     me = lax.axis_index("vocab")
     core = lax.rem(me, 2)
@@ -194,31 +210,28 @@
 
     pl.semaphore_wait(barrier, len(neighbours))
 
-    def part_rows(d, sub):
-        part = part_of_sub[sub]
-        start = d * part_block[part] + sub_start[sub] - sub_start[part_subs[part][0]]
-        return pair_parts[part].at[pl.ds(start, sub_rows[sub]), :]
-
-    def rest_rows():
-        return pair_parts[rest_part].at[pl.ds(side * part_block[rest_part], columns - side * quarter), :]
-
-    def entry_copy(sub):
-        start = pl.multiple_of(req * quarter + sub_start[sub], 16)
+    def part_rows(arrival_name):
+        part, start = part_place[arrival_name]
+        size = sub_rows[arrival_name[2]] if arrival_name[0] == "W" else rest_rows[arrival_name[1]]
+        return pair_parts[part].at[pl.ds(start, size), :]
+
+    def entry_copy(name):
+        if name[0] == "W":
+            sub = name[2]
+            start, size = pl.multiple_of(req * quarter + sub_start[sub], 16), sub_rows[sub]
+            send, recv = entry_plan[sub], weight_slot[(0, sub)]
+        else:
+            start, size = rest_start[name[1]], rest_rows[name[1]]
+            send, recv = rest_plan[name[1]], rest_slots[name[1]]
         return pltpu.make_async_remote_copy(
-            src_ref=weight_hbm.at[pl.ds(start, sub_rows[sub]), :], dst_ref=part_rows(0, sub),
-            send_sem=weight_send.at[entry_plan[sub]], recv_sem=weight_recv.at[weight_slot[(0, sub)]],
-            device_id=pair_target, device_id_type=mesh_ids)
-
-    def rest_copy():
-        return pltpu.make_async_remote_copy(
-            src_ref=weight_hbm.at[pl.ds(side * quarter, columns - side * quarter), :], dst_ref=rest_rows(),
-            send_sem=weight_send.at[rest_plan], recv_sem=weight_recv.at[rest_slot],
+            src_ref=weight_hbm.at[pl.ds(start, size), :], dst_ref=part_rows(name),
+            send_sem=weight_send.at[send], recv_sem=weight_recv.at[recv],
             device_id=pair_target, device_id_type=mesh_ids)
 
     def weight_relay(d, sub, link):
         landing = weight_landing(d, link)
         return pltpu.make_async_remote_copy(
-            src_ref=part_rows(d, sub), dst_ref=part_rows(landing, sub),
+            src_ref=part_rows(("W", d, sub)), dst_ref=part_rows(("W", landing, sub)),
             send_sem=weight_send.at[weight_plan[((d, sub), link)]], recv_sem=weight_recv.at[weight_slot[(landing, sub)]],
             device_id=z_target(1 if link == "up" else 3), device_id_type=mesh_ids)
 
@@ -254,20 +267,18 @@
             for link in taken:
                 tag_copy((p, dy), link).start()
 
-    entry_copy(0).start()
+    entry_copy(entries[0]).start()
     for piece in (0, 2, 1, 3):
         send_onward(0, 0, piece)
-    for sub in range(1, len(sub_rows)):
-        entry_copy(sub).start()
-    rest_copy().start()
-
-    weight_copy.wait()
+    for name in entries[1:]:
+        entry_copy(name).start()
 
     def arrival(event):
         if event[0] == "D":
-            pltpu.make_async_copy(rest_rows(), rest_rows(), weight_recv.at[rest_slot]).wait()
+            here = part_rows(event)
+            pltpu.make_async_copy(here, here, weight_recv.at[rest_slots[event[1]]]).wait()
         elif event[0] == "W":
-            here = part_rows(event[1], event[2])
+            here = part_rows(event)
             pltpu.make_async_copy(here, here, weight_recv.at[weight_slot[event[1:]]]).wait()
             for link in weight_links(*event[1:]):
                 weight_relay(event[1], event[2], link).start()
@@ -293,11 +304,13 @@
 
     def part_blocks(part):
         blocks = []
-        for d in range(side):
-            first = pair_first + lax.rem(req + d, side) * quarter + sub_start[part_subs[part][0]]
-            blocks.append((d * part_block[part], part_block[part], first))
-        if part == rest_part:
-            blocks.append((side * part_block[part], columns - side * quarter, pair_first + side * quarter))
+        for name in parts[part]:
+            start = part_place[name][1]
+            if name[0] == "W":
+                first = lax.rem(req + name[1], side) * quarter + sub_start[name[2]]
+                blocks.append((start, sub_rows[name[2]], pair_first + first))
+            else:
+                blocks.append((start, rest_rows[name[1]], pair_first + rest_start[name[1]]))
         return blocks
 
     def tile(group, weight_ref, blocks, fresh):
@@ -328,14 +341,40 @@
                 peak = joint
             running[group, other] = jnp.concatenate([peak, total, spread, picked] * 2, axis=0)
 
+    def at_step(step, index):
+        for event in steps[index][0]:
+            arrival(event)
+        if index == last_own_step + 1:
+            pl.semaphore_signal(token_x, inc=1, device_id=pair_target, device_id_type=mesh_ids)
+        if index == len(steps) - 3:
+            pl.semaphore_wait(token_x, 1)
+            for ahead in range(1, side):
+                pl.semaphore_signal(token_z, inc=1, device_id=z_target(ahead), device_id_type=mesh_ids)
+
+    busy_steps = [index for index in range(len(steps))
+                  if steps[index][0] or index in (last_own_step + 1, len(steps) - 3)]
+
+    def dispatch(step, low, high):
+        inside = [index for index in busy_steps if low <= index < high]
+        if not inside:
+            return
+        if len(inside) == 1:
+            @pl.when(step == inside[0])
+            def _():
+                at_step(step, inside[0])
+            return
+        middle = inside[len(inside) // 2]
+
+        @pl.when(step < middle)
+        def _():
+            dispatch(step, low, middle)
+
+        @pl.when(step >= middle)
+        def _():
+            dispatch(step, middle, high)
+
     def one_step(step, carry):
-        for index, (events, kind, group) in enumerate(steps):
-            if events:
-                @pl.when(step == index)
-                def _():
-                    for event in events:
-                        arrival(event)
-
+        dispatch(step, 0, len(steps))
         code = jnp.int32(0)
         for index, (events, kind, group) in enumerate(steps):
             code = jnp.where(step == index, kind * group_count + group, code)
@@ -347,36 +386,29 @@
             for piece in range(pieces):
                 there = rows.at[group_now, pl.ds(cap + piece * piece_rows, piece_rows), :]
                 pltpu.make_async_copy(there, there, partner_recv.at[group_now * pieces + piece]).wait()
-            landing = group_now * 2 + 1
-            pltpu.make_async_copy(tags.at[landing], tags.at[landing], tag_recv.at[landing]).wait()
+            tag_here(group_now * 2 + 1).wait()
             tile(group_now, weight_t, own_blocks, True)
 
-        for part in range(len(part_subs)):
-            @pl.when(kind_now == part + 1)
-            def _():
-                tile(group_now, pair_parts[part], part_blocks(part), False)
-
-        for index, (events, kind, group) in enumerate(steps):
-            if kind == last_part:
-                @pl.when(step == index)
+        @pl.when(kind_now > 0)
+        def _():
+            for part in range(len(parts)):
+                @pl.when(kind_now == part + 1)
                 def _():
-                    for other in range(2):
-                        if group == 0 and other == 0:
+                    tile(group_now, pair_parts[part], part_blocks(part), False)
+                    if part + 1 == last_part:
+                        where = (group_now // side, lax.rem(group_now, side))
+                        stat_copy(where, 1).start()
+
+                        @pl.when(group_now == 0)
+                        def _():
                             stats_in[my_place] = running[0, 0]
-                        else:
-                            stat_copy(all_groups[group], other).start()
-
-        @pl.when(step == last_own_step)
-        def _():
-            pl.semaphore_signal(token_x, inc=1, device_id=pair_target, device_id_type=mesh_ids)
-
-        @pl.when(step == len(steps) - 3)
-        def _():
-            pl.semaphore_wait(token_x, 1)
-            for ahead in range(1, side):
-                pl.semaphore_signal(token_z, inc=1, device_id=z_target(ahead), device_id_type=mesh_ids)
+
+                        @pl.when(group_now > 0)
+                        def _():
+                            stat_copy(where, 0).start()
         return carry
 
+    weight_copy.wait()
     lax.fori_loop(0, len(steps), one_step, 0)
 
     sources = 2 * group_count
@@ -457,9 +489,8 @@
     lax.fori_loop(0, len(row_plan), drain, 0)
     for (d, sub), link in weight_plan:
         weight_relay(d, sub, link).wait_send()
-    for sub in range(len(sub_rows)):
-        entry_copy(sub).wait_send()
-    rest_copy().wait_send()
+    for name in entries:
+        entry_copy(name).wait_send()
 
     def drain_tags(index, carry):
         pltpu.make_async_copy(tags.at[0], tags.at[0], tag_send.at[index]).wait()
@@ -485,8 +516,6 @@
     smem = pl.BlockSpec(memory_space=pltpu.SMEM)
     dma = pltpu.SemaphoreType.DMA
     regular = pltpu.SemaphoreType.REGULAR
-    part_sizes = [side * block + (columns - side * quarter if part == rest_part else 0)
-                  for part, block in enumerate(part_block)]
     out = jax.ShapeDtypeStruct((2, seq_count, seq_len), f32)
     both = pl.pallas_call(
         kernel,
@@ -507,7 +536,7 @@
             dma((group_count * pieces,)),
             dma((group_count * pieces,)),
             dma((weight_sends,)),
-            dma((rest_slot + 1,)),
+            dma((rest_slots[-1] + 1,)),
             dma((len(tag_plan),)),
             dma((2 * group_count,)),
             dma((2 * group_count,)),

time: 74.4 us -> 72.1 us (0.969)
  Pallas kernels: 72.3 us -> 70 us
    pallas_call x1, Pallas kernels: 72.3 us -> 70 us  [local(): pl.pallas_call(kernel, out_shape=out, in_specs=[smem, smem, vmem, vmem, v...]
where the time goes in v5:
time: 72.1 us; the launch traced here: 71.9 us
  Pallas kernels  70 us (97%)
  local copies, waits for them, and re-layouts  1.28 us (2%)
    pallas_call x1, Pallas kernels, local(): pl.pallas_call(kernel, out_shape=out, in_specs=[smem, smem, vmem, vmem, v...  70 us

profile of v5, /device:TPU:1, one launch (start us, length us, event | category | flops | bytes accessed | tf_op | source)
XLA Modules:
  0.0 71.9 jit_solution(5102973254630397506)
XLA Ops:
  0.6 70.0 %head_stats.1 = f32[2,8,24]{2,1,0:T(8,128)} custom-call(s32[8]{0:T(128)} %lens.1, s32[8]{0:T(128)} %slots.1, bf16[192,2048]{1,0:T(8,128)(2,1)} %hidden.1, f32[1,2048]{1,0:T(1,128)} %bitcast.8, s32[1,192]{1,0:T(1,128)} %bitcast.9, bf16[1000,2048]{1,0:T(8,128)(2,1)} %bitcast.7), custom_call_target="tpu_custom_call" | custom-call | tf_op jit(solution)/shard_map/head_stats/pallas_call | solution.py:520
  70.7 1.3 %slice_bitcast_fusion = (f32[8,24]{1,0:T(8,128)}, f32[8,24]{1,0:T(8,128)}) fusion(f32[2,8,24]{2,1,0:T(8,128)} %head_stats.1), kind=kLoop, calls=%fused_computation | loop fusion | bytes 3072 | tf_op jit(solution)/shard_map/squeeze | solution.py:552

commit v6 on v5

--- a/solution.py
+++ b/solution.py
@@ -13,42 +13,26 @@
 mesh_ids = pl.DeviceIdType.MESH
 f32 = jnp.float32
 
-sub_rows = (32, 32, 32, 32, 48, 32)
+sub_rows = (32, 32, 16, 32, 64, 32)
 rest_rows = (80, 88)
-entries = [("W", 0, 0), ("W", 0, 1), ("W", 0, 2), ("W", 0, 3), ("W", 0, 4), ("D", 0), ("W", 0, 5), ("D", 1)]
-parts = [[("W", 0, 0), ("W", 0, 1), ("W", 3, 0), ("W", 1, 0), ("W", 0, 2), ("W", 3, 1), ("W", 1, 1), ("W", 0, 3), ("W", 2, 0), ("W", 1, 2), ("W", 0, 4), ("W", 3, 2), ("W", 2, 1), ("W", 3, 3), ("W", 1, 3)], [("D", 0)], [("W", 3, 4), ("W", 1, 4), ("W", 0, 5), ("W", 2, 2), ("W", 2, 3), ("W", 1, 5), ("W", 2, 4), ("W", 3, 5), ("D", 1), ("W", 2, 5)]]
+entries = [("W", 0, 0), ("W", 0, 1), ("W", 0, 2), ("W", 0, 3), ("W", 0, 4), ("W", 0, 5), ("D", 0), ("D", 1)]
+parts = [[("W", 0, 0), ("W", 0, 1), ("W", 0, 2), ("W", 3, 0), ("W", 1, 0), ("W", 0, 3), ("W", 3, 1), ("W", 1, 1), ("W", 3, 2), ("W", 1, 2), ("W", 2, 0), ("W", 1, 3), ("W", 0, 4), ("W", 3, 3), ("W", 2, 1), ("W", 0, 5)], [("W", 2, 2), ("W", 2, 3), ("W", 3, 4), ("D", 0), ("W", 1, 4), ("W", 3, 5), ("W", 1, 5), ("W", 2, 4), ("W", 2, 5), ("D", 1)]]
 steps = [
-    ([], 0, 0),
-    ([("W", 0, 0), ("R", 1, 0, 0), ("R", 0, 3, 0), ("R", 0, 1, 0), ("W", 0, 1), ("R", 0, 3, 2), ("R", 0, 1, 2), ("R", 1, 0, 2), ("W", 3, 0), ("W", 1, 0), ("W", 0, 2), ("R", 1, 0, 1), ("R", 0, 3, 1), ("R", 0, 1, 1), ("W", 3, 1), ("W", 1, 1), ("W", 0, 3), ("R", 0, 3, 3), ("R", 0, 1, 3), ("R", 1, 0, 3)], 0, 1),
-    ([("W", 2, 0), ("W", 1, 2), ("R", 1, 3, 0), ("R", 1, 1, 0), ("R", 1, 3, 2)], 0, 3),
-    ([("W", 0, 4), ("W", 3, 2), ("W", 2, 1)], 0, 4),
-    ([("R", 0, 2, 0), ("R", 1, 1, 2), ("R", 1, 1, 1), ("W", 3, 3), ("W", 1, 3)], 1, 0),
-    ([], 1, 1),
-    ([("R", 0, 2, 2), ("R", 0, 2, 1), ("R", 1, 3, 3)], 1, 3),
-    ([], 1, 4),
-    ([("D", 0), ("R", 1, 3, 1), ("R", 1, 1, 3), ("R", 0, 2, 3)], 2, 0),
-    ([("W", 3, 4), ("W", 1, 4)], 2, 1),
-    ([], 2, 3),
-    ([], 2, 4),
-    ([], 0, 2),
-    ([("W", 0, 5), ("R", 1, 2, 0), ("R", 1, 2, 1), ("R", 1, 2, 2)], 0, 5),
-    ([("W", 2, 2), ("W", 2, 3)], 0, 7),
-    ([("R", 1, 2, 3)], 1, 2),
-    ([], 1, 5),
-    ([("W", 1, 5), ("W", 2, 4)], 0, 6),
-    ([], 1, 7),
-    ([("W", 3, 5)], 1, 6),
-    ([("D", 1)], 2, 2),
-    ([], 2, 5),
-    ([("W", 2, 5)], 2, 7),
-    ([], 2, 6),
-    ([], 3, 6),
+    ([("W", 0, 0), ("R", 1, 0, 0), ("R", 0, 3, 0), ("R", 0, 1, 0), ("W", 0, 1), ("R", 0, 3, 2), ("R", 0, 1, 2), ("R", 1, 0, 2), ("W", 0, 2), ("W", 3, 0), ("W", 1, 0), ("R", 1, 0, 1), ("R", 0, 3, 1), ("R", 0, 1, 1), ("W", 0, 3), ("W", 3, 1), ("W", 1, 1), ("R", 0, 3, 3), ("R", 0, 1, 3), ("R", 1, 0, 3), ("W", 3, 2), ("W", 1, 2)], 0, 0),
+    ([("R", 1, 3, 0), ("R", 1, 1, 0), ("R", 1, 3, 2)], 0, 1),
+    ([("W", 2, 0), ("W", 1, 3), ("W", 0, 4)], 1, 0),
+    ([("R", 0, 2, 0), ("R", 1, 1, 2), ("R", 1, 1, 1), ("W", 3, 3), ("W", 2, 1)], 1, 1),
+    ([("W", 0, 5), ("W", 2, 2)], 2, 0),
+    ([("R", 0, 2, 2), ("R", 0, 2, 1), ("R", 1, 3, 3), ("W", 2, 3)], 2, 1),
+    ([("R", 1, 3, 1), ("R", 1, 1, 3), ("R", 0, 2, 3)], 0, 2),
+    ([("W", 3, 4), ("D", 0), ("R", 1, 2, 0), ("R", 1, 2, 1), ("R", 1, 2, 2)], 1, 2),
+    ([("W", 1, 4), ("W", 3, 5)], 2, 2),
+    ([("R", 1, 2, 3), ("W", 1, 5)], 0, 3),
+    ([], 1, 3),
+    ([("W", 2, 4)], 2, 3),
+    ([("W", 2, 5), ("D", 1)], 3, 3),
     ([], 3, 2),
-    ([], 3, 5),
-    ([], 3, 7),
     ([], 3, 1),
-    ([], 3, 3),
-    ([], 3, 4),
     ([], 3, 0),
 ]
 sub_start = [sum(sub_rows[:index]) for index in range(len(sub_rows))]
@@ -108,7 +92,7 @@
     return (d + (3 if link == "up" else 1)) % side
 
 
-all_groups = [(p, dy) for p in range(2) for dy in range(side)]
+all_groups = [(0, 0), (0, 1), (0, 3), (1, 0), (1, 1), (1, 3), (0, 2), (1, 2)]
 row_plan = {}
 tag_plan = {}
 tag_first = {}
@@ -130,22 +114,22 @@
 entry_plan = {sub: len(weight_plan) + sub for sub in range(len(sub_rows))}
 rest_plan = [len(weight_plan) + len(sub_rows) + index for index in range(len(rest_rows))]
 weight_sends = rest_plan[-1] + 1
-last_part = len(parts)
+part_count = 2 + len(parts)
 last_own_step = max(index for index, step_entry in enumerate(steps) if step_entry[1] == 0)
 
 
 def kernel(lens, slots, hidden, gain, targets, weight_hbm, out, *scratch):
-    weight_t, rows, tags, running, stats_in, fin, gathered = scratch[:7]
-    pair_parts = scratch[7:7 + len(parts)]
-    (weight_sem, row_send, row_recv, partner_recv, weight_send, weight_recv, tag_send, tag_recv,
-     stat_send, stat_recv, token_x, token_z, fin_send, fin_recv) = scratch[7 + len(parts):]
+    (weights, column_ids, rows, tags, running, stats_in, fin, gathered, weight_sem, row_send, row_recv, partner_recv, weight_send, weight_recv, tag_send, tag_recv,
+     stat_send, stat_recv, token_x, token_z, fin_send, fin_recv) = scratch
     req = lax.axis_index("req")
     me = lax.axis_index("vocab")
     core = lax.rem(me, 2)
     chip_x = lax.rem(me // 2, side)
     chip_y = me // (2 * side)
     members = 2 * side * side
-    columns, depth = weight_t.shape
+    columns, depth = weight_hbm.shape
+    part_height = weights.shape[1]
+    own_sizes = (part_height, columns - part_height)
     side_x = lax.rem(chip_x, 2)
     pair_x = side - 1 - chip_x
 
@@ -174,8 +158,13 @@
     for neighbour in neighbours:
         pl.semaphore_signal(barrier, inc=1, device_id=neighbour, device_id_type=mesh_ids)
 
-    weight_copy = pltpu.make_async_copy(weight_hbm, weight_t, weight_sem)
-    weight_copy.start()
+    def own_copy(part):
+        return pltpu.make_async_copy(
+            weight_hbm.at[pl.ds(part * part_height, own_sizes[part]), :],
+            weights.at[part, pl.ds(0, own_sizes[part]), :], weight_sem.at[part])
+
+    for part in range(2):
+        own_copy(part).start()
 
     seq_count = lens.shape[0]
     held = hidden.shape[0]
@@ -213,7 +202,7 @@
     def part_rows(arrival_name):
         part, start = part_place[arrival_name]
         size = sub_rows[arrival_name[2]] if arrival_name[0] == "W" else rest_rows[arrival_name[1]]
-        return pair_parts[part].at[pl.ds(start, size), :]
+        return weights.at[2 + part, pl.ds(start, size), :]
 
     def entry_copy(name):
         if name[0] == "W":
@@ -236,7 +225,7 @@
             device_id=z_target(1 if link == "up" else 3), device_id_type=mesh_ids)
 
     def row_index(group):
-        return group[0] * side + group[1]
+        return all_groups.index(group)
 
     def piece_copy(group, piece, link):
         landing = row_index(row_landing(*group, link))
@@ -292,19 +281,20 @@
 
     my_place = (chip_y * 2 + side_x) * 2 + core
 
-    def stat_copy(group, other):
+    def stat_copy(slot, group, other):
         return pltpu.make_async_remote_copy(
-            src_ref=running.at[row_index(group), other], dst_ref=stats_in.at[my_place],
-            send_sem=stat_send.at[row_index(group) * 2 + other], recv_sem=stat_recv,
+            src_ref=running.at[slot, other], dst_ref=stats_in.at[my_place],
+            send_sem=stat_send.at[slot * 2 + other], recv_sem=stat_recv,
             device_id=(req, group_owner(group, other)), device_id_type=mesh_ids)
 
     own_first = me * columns
     pair_first = vocab_id(pair_x, chip_y, core) * columns
-    own_blocks = [(0, columns, own_first)]
 
     def part_blocks(part):
+        if part < 2:
+            return [(0, own_sizes[part], own_first + part * part_height)]
         blocks = []
-        for name in parts[part]:
+        for name in parts[part - 2]:
             start = part_place[name][1]
             if name[0] == "W":
                 first = lax.rem(req + name[1], side) * quarter + sub_start[name[2]]
@@ -313,33 +303,56 @@
                 blocks.append((start, rest_rows[name[1]], pair_first + rest_start[name[1]]))
         return blocks
 
-    def tile(group, weight_ref, blocks, fresh):
-        logits = lax.dot_general(weight_ref[...], rows[group], (((1,), (1,)), ((), ())), preferred_element_type=f32)
+    for part in range(part_count):
+        filled = 0
+        for start, size, first in part_blocks(part):
+            column_ids[part, pl.ds(start, size), :] = lax.broadcasted_iota(jnp.int32, (size, cap), 0) + first
+            filled += size
+        if filled < part_height:
+            missing = part_height - filled
+            column_ids[part, pl.ds(filled, missing), :] = jnp.full((missing, cap), -1, jnp.int32)
+            weights[part, pl.ds(filled, missing), :] = jnp.zeros((missing, depth), jnp.bfloat16)
+    empty = jnp.where(lax.rem(lax.broadcasted_iota(jnp.int32, (8, cap), 0), 4) == 0, -1e30, 0.0)
+    for group in range(group_count):
         for other in range(2):
-            piece = logits[:, other * cap:(other + 1) * cap]
+            running[group, other] = empty
+
+    sure = part_height - 8
+
+    def tile(pair, part):
+        taken = rows[pl.ds(pair * 2, 2)].reshape(4 * cap, depth)
+        logits = lax.dot_general(weights[part], taken, (((1,), (1,)), ((), ())), preferred_element_type=f32)
+        for block_index in range(4):
+            group = pair * 2 + block_index // 2
+            other = block_index % 2
+            lanes = slice(block_index * cap, (block_index + 1) * cap)
             tag = tags[group * 2 + other]
-            peak = jnp.max(piece, axis=0, keepdims=True)
-            shifted = piece - peak
+            ids_tail = column_ids[part, sure:, :]
+            main = logits[:sure, lanes]
+            tail = jnp.where(ids_tail >= 0, logits[sure:, lanes], -1e30)
+            peak = jnp.max(jnp.maximum(jnp.max(main.reshape(sure // 8, 8, cap), axis=0), tail), axis=0, keepdims=True)
+            shifted = main - peak
             exponent = jnp.exp(shifted)
-            total = jnp.sum(exponent, axis=0, keepdims=True)
-            spread = jnp.sum(exponent * shifted, axis=0, keepdims=True)
-            picked = jnp.zeros((1, cap), f32)
-            for start, size, first in blocks:
-                column = lax.broadcasted_iota(jnp.int32, (size, cap), 0)
-                block = piece[start:start + size]
-                picked = picked + jnp.sum(jnp.where(column == tag - first, block, 0.0), axis=0, keepdims=True)
-            if not fresh:
-                before = running[group, other]
-                joint = jnp.maximum(before[0:1], peak)
-                drop_before = before[0:1] - joint
-                drop = peak - joint
-                factor_before = jnp.exp(drop_before)
-                factor = jnp.exp(drop)
-                spread = factor_before * (before[2:3] + drop_before * before[1:2]) + factor * (spread + drop * total)
-                total = factor_before * before[1:2] + factor * total
-                picked = picked + before[3:4]
-                peak = joint
-            running[group, other] = jnp.concatenate([peak, total, spread, picked] * 2, axis=0)
+            shifted_tail = tail - peak
+            exponent_tail = jnp.exp(shifted_tail)
+            chosen = jnp.where(column_ids[part, :sure, :] == tag, main, 0.0)
+            chosen_tail = jnp.where(ids_tail == tag, tail, 0.0)
+
+            def summed(many, few):
+                return jnp.sum(jnp.sum(many.reshape(sure // 8, 8, cap), axis=0) + few, axis=0, keepdims=True)
+
+            total = summed(exponent, exponent_tail)
+            spread = summed(exponent * shifted, exponent_tail * shifted_tail)
+            picked = summed(chosen, chosen_tail)
+            before = running[group, other]
+            joint = jnp.maximum(before[0:1], peak)
+            drop_before = before[0:1] - joint
+            drop = peak - joint
+            factor_before = jnp.exp(drop_before)
+            factor = jnp.exp(drop)
+            spread = factor_before * (before[2:3] + drop_before * before[1:2]) + factor * (spread + drop * total)
+            total = factor_before * before[1:2] + factor * total
+            running[group, other] = jnp.concatenate([joint, total, spread, picked + before[3:4]] * 2, axis=0)
 
     def at_step(step, index):
         for event in steps[index][0]:
@@ -376,39 +389,46 @@
     def one_step(step, carry):
         dispatch(step, 0, len(steps))
         code = jnp.int32(0)
-        for index, (events, kind, group) in enumerate(steps):
-            code = jnp.where(step == index, kind * group_count + group, code)
-        kind_now = code // group_count
-        group_now = lax.rem(code, group_count)
-
-        @pl.when(kind_now == 0)
+        for index, (events, part, pair) in enumerate(steps):
+            code = jnp.where(step == index, part * side + pair, code)
+        part_now = code // side
+        pair_now = lax.rem(code, side)
+
+        @pl.when(part_now == 0)
         def _():
-            for piece in range(pieces):
-                there = rows.at[group_now, pl.ds(cap + piece * piece_rows, piece_rows), :]
-                pltpu.make_async_copy(there, there, partner_recv.at[group_now * pieces + piece]).wait()
-            tag_here(group_now * 2 + 1).wait()
-            tile(group_now, weight_t, own_blocks, True)
-
-        @pl.when(kind_now > 0)
+            for member in range(2):
+                group = pair_now * 2 + member
+                for piece in range(pieces):
+                    there = rows.at[group, pl.ds(cap + piece * piece_rows, piece_rows), :]
+                    pltpu.make_async_copy(there, there, partner_recv.at[group * pieces + piece]).wait()
+                tag_here(group * 2 + 1).wait()
+
+        tile(pair_now, part_now)
+
+        @pl.when(part_now == part_count - 1)
         def _():
-            for part in range(len(parts)):
-                @pl.when(kind_now == part + 1)
-                def _():
-                    tile(group_now, pair_parts[part], part_blocks(part), False)
-                    if part + 1 == last_part:
-                        where = (group_now // side, lax.rem(group_now, side))
-                        stat_copy(where, 1).start()
-
-                        @pl.when(group_now == 0)
-                        def _():
-                            stats_in[my_place] = running[0, 0]
-
-                        @pl.when(group_now > 0)
-                        def _():
-                            stat_copy(where, 0).start()
+            for member in range(2):
+                slot = pair_now * 2 + member
+                p = jnp.int32(0)
+                dy = jnp.int32(0)
+                for index in range(member, group_count, 2):
+                    p = jnp.where(slot == index, all_groups[index][0], p)
+                    dy = jnp.where(slot == index, all_groups[index][1], dy)
+                stat_copy(slot, (p, dy), 1).start()
+                if member == 1:
+                    stat_copy(slot, (p, dy), 0).start()
+                else:
+                    @pl.when(pair_now == 0)
+                    def _():
+                        stats_in[my_place] = running[0, 0]
+
+                    @pl.when(pair_now > 0)
+                    def _():
+                        stat_copy(slot, (p, dy), 0).start()
         return carry
 
-    weight_copy.wait()
+    for part in range(2):
+        own_copy(part).wait()
     lax.fori_loop(0, len(steps), one_step, 0)
 
     sources = 2 * group_count
@@ -516,6 +536,7 @@
     smem = pl.BlockSpec(memory_space=pltpu.SMEM)
     dma = pltpu.SemaphoreType.DMA
     regular = pltpu.SemaphoreType.REGULAR
+    part_height = max(part_sizes + [columns - max(part_sizes)])
     out = jax.ShapeDtypeStruct((2, seq_count, seq_len), f32)
     both = pl.pallas_call(
         kernel,
@@ -523,15 +544,15 @@
         in_specs=[smem, smem, vmem, vmem, vmem, pl.BlockSpec(memory_space=pl.ANY)],
         out_specs=vmem,
         scratch_shapes=[
-            pltpu.VMEM((columns, depth), jnp.bfloat16),
+            pltpu.VMEM((part_count, part_height, depth), jnp.bfloat16),
+            pltpu.VMEM((part_count, part_height, cap), jnp.int32),
             pltpu.VMEM((group_count, 2 * cap, depth), jnp.bfloat16),
             pltpu.VMEM((2 * group_count, 1, cap), jnp.int32),
             pltpu.VMEM((group_count, 2, 8, cap), f32),
             pltpu.VMEM((2 * group_count, 8, cap), f32),
             pltpu.VMEM((members * side, seq_count // 2, cap), f32),
             pltpu.VMEM((seq_count, cap), f32),
-        ] + [pltpu.VMEM((size, depth), jnp.bfloat16) for size in part_sizes] + [
-            dma,
+            dma((2,)),
             dma((len(row_plan),)),
             dma((group_count * pieces,)),
             dma((group_count * pieces,)),

time: 72.1 us -> 69.6 us (0.965)
  Pallas kernels: 70 us -> 67.5 us
    pallas_call x1, Pallas kernels: 70 us -> 67.5 us  [local(): pl.pallas_call(kernel, out_shape=out, in_specs=[smem, smem, vmem, vmem, v...]
where the time goes in v6:
time: 69.6 us; the launch traced here: 69.5 us
  Pallas kernels  67.5 us (97%)
  local copies, waits for them, and re-layouts  1.28 us (2%)
    pallas_call x1, Pallas kernels, local(): pl.pallas_call(kernel, out_shape=out, in_specs=[smem, smem, vmem, vmem, v...  67.5 us

profile of v6, /device:TPU:1, one launch (start us, length us, event | category | flops | bytes accessed | tf_op | source)
XLA Modules:
  0.0 69.5 jit_solution(10392821018632195568)
XLA Ops:
  0.6 67.5 %head_stats.1 = f32[2,8,24]{2,1,0:T(8,128)} custom-call(s32[8]{0:T(128)} %lens.1, s32[8]{0:T(128)} %slots.1, bf16[192,2048]{1,0:T(8,128)(2,1)} %hidden.1, f32[1,2048]{1,0:T(1,128)} %bitcast.8, s32[1,192]{1,0:T(1,128)} %bitcast.9, bf16[1000,2048]{1,0:T(8,128)(2,1)} %bitcast.7), custom_call_target="tpu_custom_call" | custom-call | tf_op jit(solution)/shard_map/head_stats/pallas_call | solution.py:541
  68.2 1.3 %slice_bitcast_fusion = (f32[8,24]{1,0:T(8,128)}, f32[8,24]{1,0:T(8,128)}) fusion(f32[2,8,24]{2,1,0:T(8,128)} %head_stats.1), kind=kLoop, calls=%fused_computation | loop fusion | bytes 3072 | tf_op jit(solution)/shard_map/squeeze | solution.py:573

commit v7 on v6

--- a/solution.py
+++ b/solution.py
@@ -13,18 +13,21 @@
 mesh_ids = pl.DeviceIdType.MESH
 f32 = jnp.float32
 
+own_part_sizes = (504, 496)
 sub_rows = (32, 32, 16, 32, 64, 32)
 rest_rows = (80, 88)
 entries = [("W", 0, 0), ("W", 0, 1), ("W", 0, 2), ("W", 0, 3), ("W", 0, 4), ("W", 0, 5), ("D", 0), ("D", 1)]
 parts = [[("W", 0, 0), ("W", 0, 1), ("W", 0, 2), ("W", 3, 0), ("W", 1, 0), ("W", 0, 3), ("W", 3, 1), ("W", 1, 1), ("W", 3, 2), ("W", 1, 2), ("W", 2, 0), ("W", 1, 3), ("W", 0, 4), ("W", 3, 3), ("W", 2, 1), ("W", 0, 5)], [("W", 2, 2), ("W", 2, 3), ("W", 3, 4), ("D", 0), ("W", 1, 4), ("W", 3, 5), ("W", 1, 5), ("W", 2, 4), ("W", 2, 5), ("D", 1)]]
 steps = [
-    ([("W", 0, 0), ("R", 1, 0, 0), ("R", 0, 3, 0), ("R", 0, 1, 0), ("W", 0, 1), ("R", 0, 3, 2), ("R", 0, 1, 2), ("R", 1, 0, 2), ("W", 0, 2), ("W", 3, 0), ("W", 1, 0), ("R", 1, 0, 1), ("R", 0, 3, 1), ("R", 0, 1, 1), ("W", 0, 3), ("W", 3, 1), ("W", 1, 1), ("R", 0, 3, 3), ("R", 0, 1, 3), ("R", 1, 0, 3), ("W", 3, 2), ("W", 1, 2)], 0, 0),
-    ([("R", 1, 3, 0), ("R", 1, 1, 0), ("R", 1, 3, 2)], 0, 1),
-    ([("W", 2, 0), ("W", 1, 3), ("W", 0, 4)], 1, 0),
-    ([("R", 0, 2, 0), ("R", 1, 1, 2), ("R", 1, 1, 1), ("W", 3, 3), ("W", 2, 1)], 1, 1),
-    ([("W", 0, 5), ("W", 2, 2)], 2, 0),
-    ([("R", 0, 2, 2), ("R", 0, 2, 1), ("R", 1, 3, 3), ("W", 2, 3)], 2, 1),
-    ([("R", 1, 3, 1), ("R", 1, 1, 3), ("R", 0, 2, 3)], 0, 2),
+    ([], 0, 4),
+    ([], 1, 4),
+    ([("W", 0, 0), ("R", 1, 0, 0), ("R", 0, 3, 0), ("R", 0, 1, 0), ("W", 0, 1), ("R", 0, 3, 2), ("R", 0, 1, 2), ("R", 1, 0, 2), ("W", 0, 2), ("W", 3, 0), ("W", 1, 0), ("R", 1, 0, 1), ("R", 0, 3, 1), ("R", 0, 1, 1), ("W", 0, 3), ("W", 3, 1), ("W", 1, 1), ("R", 0, 3, 3), ("R", 0, 1, 3), ("R", 1, 0, 3), ("W", 3, 2), ("W", 1, 2)], 0, 5),
+    ([], 0, 1),
+    ([("R", 1, 3, 0), ("R", 1, 1, 0), ("R", 1, 3, 2), ("W", 2, 0), ("W", 1, 3)], 1, 5),
+    ([("W", 0, 4)], 1, 1),
+    ([("R", 0, 2, 0), ("R", 1, 1, 2), ("R", 1, 1, 1), ("W", 3, 3), ("W", 2, 1), ("W", 0, 5)], 2, 0),
+    ([("W", 2, 2), ("R", 0, 2, 2), ("R", 0, 2, 1), ("R", 1, 3, 3)], 2, 1),
+    ([("W", 2, 3), ("R", 1, 3, 1), ("R", 1, 1, 3), ("R", 0, 2, 3)], 0, 2),
     ([("W", 3, 4), ("D", 0), ("R", 1, 2, 0), ("R", 1, 2, 1), ("R", 1, 2, 2)], 1, 2),
     ([("W", 1, 4), ("W", 3, 5)], 2, 2),
     ([("R", 1, 2, 3), ("W", 1, 5)], 0, 3),
@@ -114,13 +117,21 @@
 entry_plan = {sub: len(weight_plan) + sub for sub in range(len(sub_rows))}
 rest_plan = [len(weight_plan) + len(sub_rows) + index for index in range(len(rest_rows))]
 weight_sends = rest_plan[-1] + 1
-part_count = 2 + len(parts)
+own_sizes = own_part_sizes
+own_parts = len(own_sizes)
+part_count = own_parts + len(parts)
+part_height = max(own_sizes + tuple(part_sizes))
+ragged = part_height - min(own_sizes + tuple(part_sizes))
 last_own_step = max(index for index, step_entry in enumerate(steps) if step_entry[1] == 0)
 
 
 def kernel(lens, slots, hidden, gain, targets, weight_hbm, out, *scratch):
-    (weights, column_ids, rows, tags, running, stats_in, fin, gathered, weight_sem, row_send, row_recv, partner_recv, weight_send, weight_recv, tag_send, tag_recv,
+    (hidden_here, gain_here, targets_here, input_sem, weights, column_ids, rows, tags, running, stats_in, fin, gathered, weight_sem, row_send, row_recv, partner_recv, weight_send, weight_recv, tag_send, tag_recv,
      stat_send, stat_recv, token_x, token_z, fin_send, fin_recv) = scratch
+    input_copies = [pltpu.make_async_copy(source, target, input_sem.at[index]) for index, (source, target) in enumerate(
+        [(hidden, hidden_here), (gain, gain_here), (targets, targets_here)])]
+    for input_copy in input_copies:
+        input_copy.start()
     req = lax.axis_index("req")
     me = lax.axis_index("vocab")
     core = lax.rem(me, 2)
@@ -128,8 +139,6 @@
     chip_y = me // (2 * side)
     members = 2 * side * side
     columns, depth = weight_hbm.shape
-    part_height = weights.shape[1]
-    own_sizes = (part_height, columns - part_height)
     side_x = lax.rem(chip_x, 2)
     pair_x = side - 1 - chip_x
 
@@ -160,10 +169,10 @@
 
     def own_copy(part):
         return pltpu.make_async_copy(
-            weight_hbm.at[pl.ds(part * part_height, own_sizes[part]), :],
+            weight_hbm.at[pl.ds(sum(own_sizes[:part]), own_sizes[part]), :],
             weights.at[part, pl.ds(0, own_sizes[part]), :], weight_sem.at[part])
 
-    for part in range(2):
+    for part in range(own_parts):
         own_copy(part).start()
 
     seq_count = lens.shape[0]
@@ -182,15 +191,17 @@
             place = jnp.where((ahead >= 0) & (ahead < lens[seq]), ahead + offsets[seq], place)
         return place
 
+    for input_copy in input_copies:
+        input_copy.wait()
     place_row = compact_place(lax.broadcasted_iota(jnp.int32, (8, held), 1))[:1]
     pick = (lax.broadcasted_iota(jnp.int32, (cap, held), 0) == place_row).astype(f32).astype(jnp.bfloat16)
-    live = jnp.dot(pick, hidden[...], preferred_element_type=f32)
+    live = jnp.dot(pick, hidden_here[...], preferred_element_type=f32)
     inverse_rms = lax.rsqrt(jnp.mean(live * live, axis=1, keepdims=True) + eps_norm)
-    rows[0, 0:cap, :] = (live * inverse_rms * gain[...]).astype(jnp.bfloat16)
+    rows[0, 0:cap, :] = (live * inverse_rms * gain_here[...]).astype(jnp.bfloat16)
 
     place_col = compact_place(lax.broadcasted_iota(jnp.int32, (held, cap), 0))
     pick_t = (lax.broadcasted_iota(jnp.int32, (held, cap), 1) == place_col).astype(f32).astype(jnp.bfloat16)
-    wide = targets[...]
+    wide = targets_here[...]
     high = wide // 256
     digits = jnp.concatenate([high, wide - high * 256] + [jnp.zeros_like(wide)] * 14, axis=0)
     digits = digits.astype(f32).astype(jnp.bfloat16)
@@ -202,7 +213,7 @@
     def part_rows(arrival_name):
         part, start = part_place[arrival_name]
         size = sub_rows[arrival_name[2]] if arrival_name[0] == "W" else rest_rows[arrival_name[1]]
-        return weights.at[2 + part, pl.ds(start, size), :]
+        return weights.at[own_parts + part, pl.ds(start, size), :]
 
     def entry_copy(name):
         if name[0] == "W":
@@ -291,10 +302,10 @@
     pair_first = vocab_id(pair_x, chip_y, core) * columns
 
     def part_blocks(part):
-        if part < 2:
-            return [(0, own_sizes[part], own_first + part * part_height)]
+        if part < own_parts:
+            return [(0, own_sizes[part], own_first + sum(own_sizes[:part]))]
         blocks = []
-        for name in parts[part - 2]:
+        for name in parts[part - own_parts]:
             start = part_place[name][1]
             if name[0] == "W":
                 first = lax.rem(req + name[1], side) * quarter + sub_start[name[2]]
@@ -317,20 +328,23 @@
         for other in range(2):
             running[group, other] = empty
 
-    sure = part_height - 8
-
-    def tile(pair, part):
-        taken = rows[pl.ds(pair * 2, 2)].reshape(4 * cap, depth)
+    sure = part_height - ragged
+
+    def tile(first_group, count, part):
+        if count == 1:
+            taken = rows[first_group]
+        else:
+            taken = rows[pl.ds(first_group, count)].reshape(count * 2 * cap, depth)
         logits = lax.dot_general(weights[part], taken, (((1,), (1,)), ((), ())), preferred_element_type=f32)
-        for block_index in range(4):
-            group = pair * 2 + block_index // 2
+        for block_index in range(2 * count):
+            group = first_group + block_index // 2
             other = block_index % 2
             lanes = slice(block_index * cap, (block_index + 1) * cap)
             tag = tags[group * 2 + other]
             ids_tail = column_ids[part, sure:, :]
             main = logits[:sure, lanes]
             tail = jnp.where(ids_tail >= 0, logits[sure:, lanes], -1e30)
-            peak = jnp.max(jnp.maximum(jnp.max(main.reshape(sure // 8, 8, cap), axis=0), tail), axis=0, keepdims=True)
+            peak = jnp.maximum(jnp.max(main, axis=0, keepdims=True), jnp.max(tail, axis=0, keepdims=True))
             shifted = main - peak
             exponent = jnp.exp(shifted)
             shifted_tail = tail - peak
@@ -339,7 +353,7 @@
             chosen_tail = jnp.where(ids_tail == tag, tail, 0.0)
 
             def summed(many, few):
-                return jnp.sum(jnp.sum(many.reshape(sure // 8, 8, cap), axis=0) + few, axis=0, keepdims=True)
+                return jnp.sum(many, axis=0, keepdims=True) + jnp.sum(few, axis=0, keepdims=True)
 
             total = summed(exponent, exponent_tail)
             spread = summed(exponent * shifted, exponent_tail * shifted_tail)
@@ -390,20 +404,32 @@
         dispatch(step, 0, len(steps))
         code = jnp.int32(0)
         for index, (events, part, pair) in enumerate(steps):
-            code = jnp.where(step == index, part * side + pair, code)
-        part_now = code // side
-        pair_now = lax.rem(code, side)
+            code = jnp.where(step == index, part * 8 + pair, code)
+        part_now = code // 8
+        pair_now = lax.rem(code, 8)
+        first_now = jnp.where(pair_now < side, pair_now * 2, pair_now - side)
+
+        def partner_here(group):
+            for piece in range(pieces):
+                there = rows.at[group, pl.ds(cap + piece * piece_rows, piece_rows), :]
+                pltpu.make_async_copy(there, there, partner_recv.at[group * pieces + piece]).wait()
+            tag_here(group * 2 + 1).wait()
 
         @pl.when(part_now == 0)
         def _():
-            for member in range(2):
-                group = pair_now * 2 + member
-                for piece in range(pieces):
-                    there = rows.at[group, pl.ds(cap + piece * piece_rows, piece_rows), :]
-                    pltpu.make_async_copy(there, there, partner_recv.at[group * pieces + piece]).wait()
-                tag_here(group * 2 + 1).wait()
-
-        tile(pair_now, part_now)
+            partner_here(first_now)
+
+            @pl.when(pair_now < side)
+            def _():
+                partner_here(first_now + 1)
+
+        @pl.when(pair_now < side)
+        def _():
+            tile(first_now, 2, part_now)
+
+        @pl.when(pair_now >= side)
+        def _():
+            tile(first_now, 1, part_now)
 
         @pl.when(part_now == part_count - 1)
         def _():
@@ -427,7 +453,7 @@
                         stat_copy(slot, (p, dy), 0).start()
         return carry
 
-    for part in range(2):
+    for part in range(own_parts):
         own_copy(part).wait()
     lax.fori_loop(0, len(steps), one_step, 0)
 
@@ -536,14 +562,17 @@
     smem = pl.BlockSpec(memory_space=pltpu.SMEM)
     dma = pltpu.SemaphoreType.DMA
     regular = pltpu.SemaphoreType.REGULAR
-    part_height = max(part_sizes + [columns - max(part_sizes)])
     out = jax.ShapeDtypeStruct((2, seq_count, seq_len), f32)
     both = pl.pallas_call(
         kernel,
         out_shape=out,
-        in_specs=[smem, smem, vmem, vmem, vmem, pl.BlockSpec(memory_space=pl.ANY)],
+        in_specs=[smem, smem] + [pl.BlockSpec(memory_space=pl.ANY)] * 4,
         out_specs=vmem,
         scratch_shapes=[
+            pltpu.VMEM((held, depth), jnp.bfloat16),
+            pltpu.VMEM((1, depth), f32),
+            pltpu.VMEM((1, held), jnp.int32),
+            dma((3,)),
             pltpu.VMEM((part_count, part_height, depth), jnp.bfloat16),
             pltpu.VMEM((part_count, part_height, cap), jnp.int32),
             pltpu.VMEM((group_count, 2 * cap, depth), jnp.bfloat16),
@@ -552,7 +581,7 @@
             pltpu.VMEM((2 * group_count, 8, cap), f32),
             pltpu.VMEM((members * side, seq_count // 2, cap), f32),
             pltpu.VMEM((seq_count, cap), f32),
-            dma((2,)),
+            dma((own_parts,)),
             dma((len(row_plan),)),
             dma((group_count * pieces,)),
             dma((group_count * pieces,)),

time: 69.6 us -> 68.2 us (0.980)
  Pallas kernels: 67.5 us -> 66.1 us
    pallas_call x1, Pallas kernels: 67.5 us -> 66.1 us  [local(): pl.pallas_call(kernel, out_shape=out, in_specs=[smem, smem] + [pl.BlockSp...]
where the time goes in v7:
time: 68.2 us; the launch traced here: 68 us
  Pallas kernels  66.1 us (97%)
  local copies, waits for them, and re-layouts  1.28 us (2%)
    pallas_call x1, Pallas kernels, local(): pl.pallas_call(kernel, out_shape=out, in_specs=[smem, smem] + [pl.BlockSp...  66.1 us

profile of v7, /device:TPU:1, one launch (start us, length us, event | category | flops | bytes accessed | tf_op | source)
XLA Modules:
  0.0 68.0 jit_solution(15299474206684239863)
XLA Ops:
  0.6 66.1 %head_stats.1 = f32[2,8,24]{2,1,0:T(8,128)} custom-call(s32[8]{0:T(128)} %lens.1, s32[8]{0:T(128)} %slots.1, bf16[192,2048]{1,0:T(8,128)(2,1)} %hidden.1, f32[1,2048]{1,0:T(1,128)} %bitcast.8, s32[1,192]{1,0:T(1,128)} %bitcast.9, bf16[1000,2048]{1,0:T(8,128)(2,1)} %bitcast.7), custom_call_target="tpu_custom_call" | custom-call | tf_op jit(solution)/shard_map/head_stats/pallas_call | solution.py:566
  66.7 1.3 %slice_bitcast_fusion = (f32[8,24]{1,0:T(8,128)}, f32[8,24]{1,0:T(8,128)}) fusion(f32[2,8,24]{2,1,0:T(8,128)} %head_stats.1), kind=kLoop, calls=%fused_computation | loop fusion | bytes 3072 | tf_op jit(solution)/shard_map/squeeze | solution.py:602

commit v8 on v7

--- a/solution.py
+++ b/solution.py
@@ -36,7 +36,8 @@
     ([("W", 2, 5), ("D", 1)], 3, 3),
     ([], 3, 2),
     ([], 3, 1),
-    ([], 3, 0),
+    ([], 3, 5),
+    ([], 3, 4),
 ]
 sub_start = [sum(sub_rows[:index]) for index in range(len(sub_rows))]
 quarter = sum(sub_rows)
@@ -433,24 +434,31 @@
 
         @pl.when(part_now == part_count - 1)
         def _():
-            for member in range(2):
-                slot = pair_now * 2 + member
+            def send_stats(slot, may_be_own):
                 p = jnp.int32(0)
                 dy = jnp.int32(0)
-                for index in range(member, group_count, 2):
+                for index in range(group_count):
                     p = jnp.where(slot == index, all_groups[index][0], p)
                     dy = jnp.where(slot == index, all_groups[index][1], dy)
                 stat_copy(slot, (p, dy), 1).start()
-                if member == 1:
+                if not may_be_own:
                     stat_copy(slot, (p, dy), 0).start()
-                else:
-                    @pl.when(pair_now == 0)
-                    def _():
-                        stats_in[my_place] = running[0, 0]
-
-                    @pl.when(pair_now > 0)
-                    def _():
-                        stat_copy(slot, (p, dy), 0).start()
+                    return
+
+                @pl.when(slot == 0)
+                def _():
+                    stats_in[my_place] = running[0, 0]
+
+                @pl.when(slot > 0)
+                def _():
+                    stat_copy(slot, (p, dy), 0).start()
+
+            send_stats(first_now, True)
+
+            @pl.when(pair_now < side)
+            def _():
+                send_stats(first_now + 1, False)
+
         return carry
 
     for part in range(own_parts):

time: 68.2 us -> 67.5 us (0.990)
  Pallas kernels: 66.1 us -> 65.4 us
where the time goes in v8:
time: 67.5 us; the launch traced here: 67.3 us
  Pallas kernels  65.4 us (97%)
  local copies, waits for them, and re-layouts  1.28 us (2%)
    pallas_call x1, Pallas kernels, local(): pl.pallas_call(kernel, out_shape=out, in_specs=[smem, smem] + [pl.BlockSp...  65.4 us

profile of v8, /device:TPU:1, one launch (start us, length us, event | category | flops | bytes accessed | tf_op | source)
XLA Modules:
  0.0 67.3 jit_solution(11768505150542140495)
XLA Ops:
  0.6 65.4 %head_stats.1 = f32[2,8,24]{2,1,0:T(8,128)} custom-call(s32[8]{0:T(128)} %lens.1, s32[8]{0:T(128)} %slots.1, bf16[192,2048]{1,0:T(8,128)(2,1)} %hidden.1, f32[1,2048]{1,0:T(1,128)} %bitcast.8, s32[1,192]{1,0:T(1,128)} %bitcast.9, bf16[1000,2048]{1,0:T(8,128)(2,1)} %bitcast.7), custom_call_target="tpu_custom_call" | custom-call | tf_op jit(solution)/shard_map/head_stats/pallas_call | solution.py:574
  66.1 1.3 %slice_bitcast_fusion = (f32[8,24]{1,0:T(8,128)}, f32[8,24]{1,0:T(8,128)}) fusion(f32[2,8,24]{2,1,0:T(8,128)} %head_stats.1), kind=kLoop, calls=%fused_computation | loop fusion | bytes 3072 | tf_op jit(solution)/shard_map/squeeze | solution.py:610
